TPU v7x, 32 devices: a whole 2x2x4 slice. The times are simulated.
32 devices in a mesh: bucket: 8 (over y, x, core), rel: 4 (over z).
Axes of the slice: x: 2, y: 2, z: 4, core: 2. Of those that a mesh axis runs over, the one named last changes fastest.
Arguments:
- src_feat: bfloat16 [2048, 768], P(('bucket', 'rel')), may hold values from -22 to 22
- tgt_feat: bfloat16 [4096, 768], P(('bucket', 'rel')), may hold values from -22 to 22
- enc_weight: bfloat16 [768, 512], replicated, may hold values from -0.21875 to 0.21875
- rel_shift: bfloat16 [12, 512], P('rel'), may hold values from -3 to 3
- edge_src: int32 [8, 4, 4, 768], P('bucket', 'rel'), may hold values from 0 to 255
- edge_tgt: int32 [8, 4, 4, 768], P('bucket', 'rel'), may hold values from 0 to 511
- rel_hot: int32 [8, 4, 4, 3, 768], P('bucket', 'rel'), may hold values from 0 to 1, as said below
- neg_idx: int32 [8, 4, 4, 128], P('bucket', 'rel'), may hold values from 0 to 511
- edge_label: int32 [8, 4, 4, 768], P('bucket', 'rel'), may hold values 0 or 1
Outputs:
- src_grad: float32 [2048, 512], P(('bucket', 'rel'))
- tgt_grad: float32 [4096, 512], P(('bucket', 'rel'))
- rel_grad: float32 [12, 512], P('rel')
- enc_grad: float32 [768, 512], replicated
Inputs may be any that keep to these rules, and one draw needn't show every extreme that they name: `rel_hot`: for each edge exactly one of the three entries is 1.
All inputs are finite; a program needn't handle non-finite values. No bound on the sum of `edge_label` on one device may be relied on, other than what follows from the above.
Results may differ from a plain program's by a relative error of at most 0.00065.
The roundings to bfloat16 on the way count: a program that leaves them out, or rounds other values in their place, can miss the bound.
Values may be sent and summed in bfloat16 or wider, within the bound.
No kernel may reach another device: no remote copies, remote signals or barrier semaphores. Data moves between devices by JAX's collectives and lax.ppermute only.
A program may use at most 64 MiB of HBM per device.

v0:
```python
import functools

import jax
import jax.numpy as jnp
from jax import lax
from jax.experimental import pallas as pl
from jax.experimental.pallas import tpu as pltpu
from jax.sharding import PartitionSpec as P


LABELLED = 1024.0
LOG2E = 1.4426950408889634
SLOT_OF = (0, 1, 3, 2)
APART = (0, 2, 1, 3)
NT = (((1,), (1,)), ((), ()))
NN = (((1,), (0,)), ((), ()))
F32 = jnp.float32
BF16 = jnp.bfloat16
VMEM = pl.BlockSpec(memory_space=pltpu.VMEM)
ANY = pl.BlockSpec(memory_space=pl.ANY)


def dot(a, b, dims):
    return lax.dot_general(a, b, dims, preferred_element_type=F32)


def call(body, outs, ins, in_specs=None, scratch=(), flops=0):
    moved = sum(x.size * x.dtype.itemsize for x in ins)
    moved += sum(o.size * o.dtype.itemsize for o in outs)
    return pl.pallas_call(
        body,
        out_shape=tuple(outs),
        in_specs=in_specs or [VMEM] * len(ins),
        out_specs=tuple(VMEM for _ in outs),
        scratch_shapes=scratch,
        cost_estimate=pl.CostEstimate(flops=int(flops), bytes_accessed=int(moved), transcendentals=0),
    )(*ins)


def shaped(shape, dtype=F32):
    return jax.ShapeDtypeStruct(tuple(shape), dtype)


def field_starts(edges, negs):
    starts, at = {}, 0
    for key, size in (
        ("src", edges), ("tlo", edges), ("thi", edges), ("rel", edges), ("lab", edges), ("nlo", negs), ("nhi", negs),
    ):
        starts[key] = (at, size)
        at += size
    return starts, at


def task_rows(edges, negs, width):
    total = field_starts(edges, negs)[1]
    return -(-total // width // 8) * 8 if total % width == 0 else (-(-(-(-total // width)) // 8)) * 8


def pack(fields, rows, src, tgt, rel, neg, lab, flat):
    slots = src.shape[2]
    width = flat.shape[1]
    flat[...] = jnp.zeros_like(flat)
    for m in range(slots):
        tgt_f = tgt[0, 0, m : m + 1, :].astype(F32)
        neg_f = neg[0, 0, m : m + 1, :].astype(F32)
        t_hi = jnp.floor(tgt_f * (1.0 / 256))
        n_hi = jnp.floor(neg_f * (1.0 / 256))
        values = {
            "src": src[0, 0, m : m + 1, :].astype(F32), "tlo": tgt_f - 256.0 * t_hi, "thi": t_hi,
            "rel": rel[m : m + 1, :].astype(F32), "lab": lab[0, 0, m : m + 1, :].astype(F32),
            "nlo": neg_f - 256.0 * n_hi, "nhi": n_hi,
        }
        for key, (at, size) in fields.items():
            done = 0
            while done < size:
                row, col = divmod(at + done, width)
                n = min(width - col, size - done)
                flat[m * rows + row : m * rows + row + 1, col : col + n] = values[key][:, done : done + n]
                done += n


def first_body(fields, rows, src_feat, tgt_feat, weight, src, tgt, rel, neg, lab, shift, out, act, feats, flat):
    pack(fields, rows, src, tgt, rel, neg, lab, flat)
    n = src_feat.shape[0]
    value = jnp.tanh(dot(src_feat[...], weight[...], NN))
    act[...] = value
    out[:n, :] = value.astype(BF16)
    tasks = flat.shape[0]
    out[n : n + tasks, :] = flat[...].astype(BF16)
    out[n + tasks :, :] = jnp.zeros_like(out[n + tasks :, :])
    out[n + tasks : n + tasks + shift.shape[0], :] = shift[...]
    feats[:n, :] = src_feat[...]
    feats[n:, :] = tgt_feat[...]


def take(block, fields, key):
    at, size = fields[key]
    width = block.shape[1]
    pieces, done = [], 0
    while done < size:
        row, col = divmod(at + done, width)
        n = min(width - col, size - done)
        pieces.append(block[row : row + 1, col : col + n])
        done += n
    return pieces[0] if len(pieces) == 1 else jnp.concatenate(pieces, axis=1)


def wrapped(value, base, count):
    moved = value - base
    return jnp.where(moved < 0, moved + count, moved)


def one_hot(rows, ids, value=None):
    one = jnp.full(ids.shape, 1.0, BF16) if value is None else value.astype(BF16)
    pieces = []
    for base in range(0, rows, 256):
        n = min(256, rows - base)
        local = jnp.where((ids >= base) & (ids < base + n), ids - base, -1.0).astype(BF16)
        iota = lax.broadcasted_iota(jnp.int32, (n, ids.shape[1]), 0).astype(F32).astype(BF16)
        pieces.append(jnp.where(iota == local, one, jnp.zeros_like(one)))
    return pieces[0] if len(pieces) == 1 else jnp.concatenate(pieces, axis=0)


def own_quarter(size):
    me = lax.axis_index("bucket")
    return (me & 1) * 2 + ((me >> (size.bit_length() - 2)) & 1)


def own_half():
    return (lax.axis_index("bucket") >> 1) & 1


def aligned(number, size, base=0):
    return pl.ds(pl.multiple_of(base + number * size, size), size)


def prepare_body(size, s_rows, own, low, high, far, weight, emb, act, turned, held):
    t_rows = own.shape[0] - s_rows
    me = own_quarter(size)
    for j, x in enumerate((own, low, high, far)):
        held[aligned(me ^ APART[j], s_rows), :] = x[:s_rows, :]
        held[pl.ds(pl.multiple_of(4 * s_rows + (me ^ APART[j]) * t_rows, s_rows), t_rows), :] = x[s_rows:, :]
        emb[j * t_rows : (j + 1) * t_rows, :] = jnp.tanh(dot(x[s_rows:, :], weight[...], NN)).astype(BF16)
    columns = weight[:, aligned(me, act.shape[1])]
    act[...] = jnp.tanh(dot(held[4 * s_rows :, :], columns, NN))
    turned[...] = held[...].astype(F32).T.astype(BF16)


def start_all(copies, sems):
    started = [pltpu.make_async_copy(a, b, sems.at[i]) for i, (a, b) in enumerate(copies)]
    for c in started:
        c.start()
    for c in started:
        c.wait()


def spread(pieces, targets):
    own, plus, minus, far_a, far_b = pieces
    copies = []
    half = far_a.shape[0]
    for place, parts in ((0, ((own, 0),)), (1, ((plus, 0),)), (2, ((far_a, 0), (far_b, half))), (3, ((minus, 0),))):
        for lo, hi, ref in targets(place):
            for part, base in parts:
                a, b = max(lo, base), min(hi, base + part.shape[0])
                if a < b:
                    copies.append((part.at[pl.ds(a - base, b - a)], ref.at[pl.ds(a - lo, b - a)]))
    return copies


def weights_of(scores, coded, pairs, scale):
    sig = 1.0 / (1.0 + jnp.exp2(scores * (-scale * LOG2E)))
    labels = jnp.floor(coded * (1.0 / LABELLED))
    edges = coded - (LABELLED - 1.0) * labels
    return edges * sig - labels + pairs * sig.astype(BF16).astype(F32)


def meets_body(cfg, own, plus, minus, far_a, far_b, tgt, *refs):
    fields, rows, s_rows, t_rows, n_rel, scale, groups, negs, size = cfg
    t_outs, s_keep, s_send = refs[:4], refs[4], refs[5]
    src, idx, query, parts, acc, w_src, w_rel, total, sems = refs[6:]
    ring = lax.axis_index("rel")
    tasks = idx.shape[1] - 16

    def places(place):
        return (0, s_rows, src.at[pl.ds(place * s_rows, s_rows)]), (s_rows, own.shape[0], idx.at[place])

    start_all(spread((own, plus, minus, far_a, far_b), places), sems)
    for ref in (acc, w_src, w_rel):
        ref[...] = jnp.zeros_like(ref)
    all_src = src.shape[0]
    all_tgt = t_rows * groups
    src_base = (ring * s_rows).astype(F32)
    tgt_base = (ring * t_rows).astype(F32)
    lane = lax.broadcasted_iota(jnp.int32, (t_rows, w_rel.shape[1]), 1)

    def step(group, carry):
        shift = idx[group, tasks : tasks + 16, :]
        place = lax.rem(group + ring, groups) * n_rel
        for k in range(n_rel):
            query[k * all_src : (k + 1) * all_src, :] = src[...] + shift[k : k + 1, :]
        scores = dot(tgt[...], query[...], NT)
        for j, slot in enumerate(SLOT_OF):
            block = idx[group, slot * rows : (slot + 1) * rows, :].astype(F32)
            who = wrapped(take(block, fields, "src"), src_base, float(all_src))
            rel = take(block, fields, "rel")
            ids = wrapped(take(block, fields, "thi") * 256.0 + take(block, fields, "tlo"), tgt_base, float(all_tgt))
            weight = 1.0 + (LABELLED - 1.0) * take(block, fields, "lab")
            left = [one_hot(t_rows, jnp.where(rel == float(k), ids, -1.0), weight) for k in range(n_rel)]
            left.append(one_hot(16, rel))
            counts = dot(jnp.concatenate(left, axis=0), one_hot(all_src, who), NT)
            neg = wrapped(take(block, fields, "nhi") * 256.0 + take(block, fields, "nlo"), tgt_base, float(all_tgt))
            neg_count = jnp.sum(one_hot(t_rows, neg).astype(F32), axis=1, keepdims=True) * (1.0 / negs)
            mine = slice(j * t_rows, (j + 1) * t_rows)
            part, line = None, jnp.zeros((t_rows, w_rel.shape[1]), F32)
            for k in range(n_rel):
                top = k * t_rows
                each = n_rel * t_rows + k
                lanes = slice(k * all_src, (k + 1) * all_src)
                value = weights_of(
                    scores[mine, lanes], counts[top : top + t_rows, :], neg_count * counts[each : each + 1, :], scale
                )
                high = value.astype(BF16)
                parts[2 * j * t_rows : (2 * j + 1) * t_rows, lanes] = high
                parts[(2 * j + 1) * t_rows : (2 * j + 2) * t_rows, lanes] = (value - high.astype(F32)).astype(BF16)
                part = value if part is None else part + value
                line = jnp.where(lane == place + k, jnp.sum(value, axis=1, keepdims=True), line)
            w_src[mine, :] += part
            w_rel[mine, :] += line
        acc[...] += dot(parts[...], query[...], NN)
        return carry

    lax.fori_loop(0, groups, step, 0)
    whole = jnp.concatenate([w_src[...].T, w_rel[...].T[:16, :]], axis=0)
    high = whole.astype(BF16)
    low = (whole - high.astype(F32)).astype(BF16)
    total[...] = scale * (dot(high, tgt[...], NN) + dot(low, tgt[...], NN))
    for r in range(groups):
        out = s_send if r % 2 else s_keep
        place = lax.rem((ring ^ r) - ring + groups, groups)
        out[(r // 2) * s_rows : (r // 2 + 1) * s_rows, :] = total[aligned(place, s_rows), :]
    me = own_quarter(size)
    for i, out in enumerate(t_outs):
        lanes = aligned(me ^ APART[i], out.shape[1])
        for j in range(4):
            high, low = acc[2 * j * t_rows : (2 * j + 1) * t_rows, lanes], acc[(2 * j + 1) * t_rows : (2 * j + 2) * t_rows, lanes]
            out[aligned(me ^ APART[j], t_rows), :] = scale * (high + low)
        out[4 * t_rows :, :] = total[all_src:, lanes]


def source_body(size, keep, recv, last, act, grad, *outs):
    n = grad.shape[0]
    value = (keep[:n, :] + recv[:n, :]) + last[...]
    grad[...] = value
    d = (value * (1.0 - act[...] * act[...])).astype(BF16)
    wide = outs[0].shape[1]
    me = own_quarter(size)
    for a in range(4):
        for j, out in enumerate(outs):

            @pl.when((me ^ APART[j]) == a)
            def _():
                out[...] = d[:, a * wide : (a + 1) * wide]


def target_body(size, keep, recv, last, act, turned, *outs):
    parts, rows = outs[:2], outs[2:]
    value = (keep[...] + recv[...]) + last[...]
    n = act.shape[0]
    d = (value[:n, :] * (1.0 - act[...] * act[...])).astype(BF16)
    block = turned.shape[0] // 2
    first = turned.shape[1] - n
    for r, out in enumerate(parts):
        out[:block, :] = dot(turned[aligned(own_half() ^ r, block), first:], d, NN)
        out[block:, :] = value[n:, :]
    me = own_quarter(size)
    for a in range(4):
        for j, out in enumerate(rows):

            @pl.when((me ^ APART[j]) == a)
            def _():
                out[...] = value[a * (n // 4) : (a + 1) * (n // 4), :]


def join_body(size, keep_in, send_in, turned, *refs):
    pieces, (keep, send), held = refs[:4], refs[4:6], refs[6]
    n = pieces[0].shape[0]
    me = own_quarter(size)
    for j, x in enumerate(pieces):
        held[aligned(me ^ APART[j], n), :] = x[...]
    block = turned.shape[0] // 2
    for r, (x, out) in enumerate(((keep_in, keep), (send_in, send))):
        out[:block, :] = x[:block, :] + dot(turned[aligned(own_half() ^ r, block), : 4 * n], held[...], NN)
        out[block:, :] = x[block:, :]


def rows_body(size, *refs):
    parts, (grad,) = refs[:4], refs[4:]
    me = own_quarter(size)
    for j, x in enumerate(parts):
        grad[:, aligned(me ^ APART[j], x.shape[1])] = x[...]


def place_body(size, *refs):
    blocks, (enc_grad, rel_grad) = refs[:8], refs[8:]
    block = enc_grad.shape[0] // 2
    me = own_quarter(size)
    n_rel = rel_grad.shape[0]
    for r in range(2):
        for j in range(4):
            x = blocks[r * 4 + j]
            lanes = aligned(me ^ APART[j], x.shape[1])
            enc_grad[aligned(own_half() ^ r, block), lanes] = x[:block, :]
            if r == 0:
                for k in range(n_rel):
                    rel_grad[k : k + 1, lanes] = x[pl.ds(block + lax.axis_index("rel") * n_rel + k, 1), :]


def shards(src_feat, tgt_feat, enc_weight, rel_shift, edge_src, edge_tgt, rel_hot, neg_idx, edge_label):
    buckets = lax.axis_size("bucket")
    groups = lax.axis_size("rel")
    half = buckets // 2
    s_rows, t_rows = src_feat.shape[0], tgt_feat.shape[0]
    feat, emb = enc_weight.shape
    slots, edges = edge_src.shape[2:]
    negs = neg_idx.shape[3]
    n_rel = rel_hot.shape[3]
    fields, _ = field_starts(edges, negs)
    rows = task_rows(edges, negs, emb)
    cfg = (fields, rows, s_rows, t_rows, n_rel, emb**-0.5, groups, negs, buckets)
    n = s_rows + t_rows
    wide = emb // 4

    def met(x, mask):
        return lax.ppermute(x, "bucket", [(i, i ^ mask) for i in range(buckets)])

    def ring(x, step):
        return lax.ppermute(x, "rel", [(i, (i - step) % groups) for i in range(groups)])

    def crossed(x, mask):
        return lax.ppermute(x, "rel", [(i, i ^ mask) for i in range(groups)])

    def around(x):
        cut_at = x.shape[0] // 2
        plus, minus = ring(x, 1), ring(x, -1)
        return x, plus, minus, ring(plus[:cut_at], 1), ring(minus[cut_at:], -1)

    def shared(parts):
        return [parts[0], met(parts[1], 1), met(parts[2], half), met(parts[3], half + 1)]

    which = sum(k * rel_hot[0, 0, :, k, :] for k in range(1, n_rel))
    own, s_act, feats = call(
        functools.partial(first_body, fields, rows),
        [shaped((s_rows + slots * rows + 16, emb), BF16), shaped((s_rows, emb)), shaped((n, feat), BF16)],
        [src_feat, tgt_feat, enc_weight, edge_src, edge_tgt, which, neg_idx, edge_label, rel_shift],
        scratch=[pltpu.VMEM((slots * rows, emb), F32)],
        flops=2 * s_rows * feat * emb,
    )
    first = around(own)
    f_high = met(feats, half)
    f_low = met(feats, 1)
    f_far = met(f_high, 1)
    tgt, act, turned = call(
        functools.partial(prepare_body, buckets, s_rows),
        [shaped((4 * t_rows, emb), BF16), shaped((4 * t_rows, wide)), shaped((feat, 4 * n), BF16)],
        [feats, f_low, f_high, f_far, enc_weight],
        scratch=[pltpu.VMEM((4 * n, feat), BF16)],
        flops=8 * n * feat * emb,
    )
    queries = n_rel * groups * s_rows
    *t_parts, s_keep, s_send = call(
        functools.partial(meets_body, cfg),
        [shaped((4 * t_rows + 16, wide))] * 4 + [shaped((groups // 2 * s_rows, emb))] * 2,
        [*first, tgt],
        in_specs=[ANY] * 5 + [VMEM],
        scratch=[
            pltpu.VMEM((groups * s_rows, emb), BF16),
            pltpu.VMEM((groups, slots * rows + 16, emb), BF16),
            pltpu.VMEM((queries, emb), BF16),
            pltpu.VMEM((8 * t_rows, queries), BF16),
            pltpu.VMEM((8 * t_rows, emb), F32),
            pltpu.VMEM((4 * t_rows, groups * s_rows), F32),
            pltpu.VMEM((4 * t_rows, 128), F32),
            pltpu.VMEM((groups * s_rows + 16, emb), F32),
            pltpu.SemaphoreType.DMA((32,)),
        ],
        flops=12e9,
    )
    s_recv = crossed(s_send, 1)
    t_recv, t_next = met(t_parts[1], 1), met(t_parts[3], 1)
    t_last = met(t_parts[2] + t_next, half)
    s_last = crossed(s_keep[s_rows:] + s_recv[s_rows:], 2)
    part = feat // 2
    keep, send, *g_parts = call(
        functools.partial(target_body, buckets),
        [shaped((part + 16, wide))] * 2 + [shaped((t_rows, wide))] * 4,
        [t_parts[0], t_recv, t_last, act, turned],
        flops=8 * t_rows * feat * wide,
    )
    keep, send, s_last = lax.optimization_barrier((keep, send, s_last))
    src_grad, *d_parts = call(
        functools.partial(source_body, buckets),
        [shaped((s_rows, emb))] + [shaped((s_rows, wide), BF16)] * 4,
        [s_keep, s_recv, s_last, s_act],
    )
    keep, send = call(
        functools.partial(join_body, buckets),
        [shaped((part + 16, wide))] * 2,
        [keep, send, turned, *shared(d_parts)],
        scratch=[pltpu.VMEM((4 * s_rows, wide), BF16)],
        flops=8 * s_rows * feat * wide,
    )
    got = met(send, 2)
    g_parts, got = lax.optimization_barrier((shared(g_parts), got))
    joint = keep + got
    (tgt_grad,) = call(functools.partial(rows_body, buckets), [shaped((t_rows, emb))], g_parts)
    for bit in range(2, buckets.bit_length() - 2):
        joint = joint + met(joint, 1 << bit)
    got = crossed(joint, 1)
    tgt_grad, got = lax.optimization_barrier((tgt_grad, got))
    joint = joint + got
    joint = joint + crossed(joint, 3)
    same = [joint, met(joint, half), met(joint, 2), met(joint, half + 2)]
    other = [met(x, 1) for x in same]
    blocks = [same[0], other[0], same[1], other[1], same[2], other[2], same[3], other[3]]
    enc_grad, rel_grad = call(
        functools.partial(place_body, buckets), [shaped((feat, emb)), shaped((n_rel, emb))], blocks
    )
    return (src_grad, tgt_grad, rel_grad, enc_grad)


def solution(mesh):
    in_specs = (
        P(("bucket", "rel"), None),
        P(("bucket", "rel"), None),
        P(),
        P("rel", None),
        P("bucket", "rel", None, None),
        P("bucket", "rel", None, None),
        P("bucket", "rel", None, None, None),
        P("bucket", "rel", None, None),
        P("bucket", "rel", None, None),
    )
    out_specs = (P(("bucket", "rel"), None), P(("bucket", "rel"), None), P("rel", None), P())

    return jax.shard_map(shards, mesh=mesh, in_specs=in_specs, out_specs=out_specs, check_vma=False)
```

profile of v0, /device:TPU:0, one launch (start us, length us, event | category | flops | bytes accessed | tf_op | source)
XLA Modules:
  0.0 116.8 jit_solution(3396071700435219510)
XLA Ops:
  0.6 1.3 %add_bitcast_fusion.rel = s32[4,768]{1,0:T(4,128)} fusion(s32[1,1,4,3,768]{4,2,3,1,0:T(4,128)} %param.15), kind=kLoop, calls=%fused_computation.1 | loop fusion | flops 6144 | bytes 36864 | tf_op jit(solution)/shard_map/add | solution.py:350
  2.0 2.4 %shard_map.120 = (bf16[112,512]{1,0:T(8,128)(2,1)}, f32[64,512]{1,0:T(8,128)}, bf16[192,768]{1,0:T(8,128)(2,1)}) custom-call(bf16[64,768]{1,0:T(8,128)(2,1)} %src_feat.1, bf16[128,768]{1,0:T(8,128)(2,1)} %tgt_feat.1, bf16[768,512]{1,0:T(8,128)(2,1)} %weight.3, s32[1,1,4,768]{3,2,1,0:T(4,128)} %src.1, s32[1,1,4,768]{3,2,1,0:T(4,128)} %tgt.1, ...), custom_call_target="tpu_custom_call" | custom-call | flops 50331648 | bytes 1676288 | tf_op jit(solution)/shard_map/pallas_call | solution.py:30
  4.4 3.0 %collective-permute-start.5 = (bf16[192,768]{1,0:T(8,128)(2,1)}, bf16[192,768]{1,0:T(8,128)(2,1)S(1)}, u32[]{:S(2)}, u32[]{:S(2)}) collective-permute-start(bf16[192,768]{1,0:T(8,128)(2,1)} %get-tuple-element.42.own), channel_id=1, source_target_pairs={{0,16},{4,20},{8,24},{12,28},{16,0},{20,4},{24,8},{28,12},{1,17},{... | collective-permute-start | bytes 884744 | tf_op jit(solution)/shard_map/ppermute | solution.py:334
  7.4 0.0 collective-permute-start.4
  7.4 7.2 %collective-permute-done.5.high = bf16[192,768]{1,0:T(8,128)(2,1)S(1)} collective-permute-done((bf16[192,768]{1,0:T(8,128)(2,1)}, bf16[192,768]{1,0:T(8,128)(2,1)S(1)}, u32[]{:S(2)}, u32[]{:S(2)}) %collective-permute-start.5) | collective-permute-done | bytes 294944 | tf_op jit(solution)/shard_map/ppermute | solution.py:334
  14.6 0.0 collective-permute-start.6
  14.6 1.8 %collective-permute-start.1 = (bf16[112,512]{1,0:T(8,128)(2,1)}, bf16[112,512]{1,0:T(8,128)(2,1)S(1)}, u32[]{:S(2)}, u32[]{:S(2)}) collective-permute-start(bf16[112,512]{1,0:T(8,128)(2,1)} %get-tuple-element.41.own), channel_id=1, source_target_pairs={{0,1},{1,2},{2,3},{3,0},{4,5},{5,6},{6,7},{7,4},{8,9},{9,10},{10,1... | collective-permute-start | bytes 344072 | tf_op jit(solution)/shard_map/ppermute | solution.py:337
  16.4 2.1 %collective-permute-start = (bf16[112,512]{1,0:T(8,128)(2,1)}, bf16[112,512]{1,0:T(8,128)(2,1)S(1)}, u32[]{:S(2)}, u32[]{:S(2)}) collective-permute-start(bf16[112,512]{1,0:T(8,128)(2,1)} %get-tuple-element.41.own), channel_id=1, source_target_pairs={{0,3},{1,0},{2,1},{3,2},{4,7},{5,4},{6,5},{7,6},{8,11},{9,8},{10,9... | collective-permute-start | bytes 344072 | tf_op jit(solution)/shard_map/ppermute | solution.py:337
  18.5 4.2 %collective-permute-done.1.minus = bf16[112,512]{1,0:T(8,128)(2,1)S(1)} collective-permute-done((bf16[112,512]{1,0:T(8,128)(2,1)}, bf16[112,512]{1,0:T(8,128)(2,1)S(1)}, u32[]{:S(2)}, u32[]{:S(2)}) %collective-permute-start.1) | collective-permute-done | bytes 114720 | tf_op jit(solution)/shard_map/ppermute | solution.py:337
  22.7 0.1 collective-permute-start.3
  22.7 1.6 %collective-permute-done.plus = bf16[112,512]{1,0:T(8,128)(2,1)S(1)} collective-permute-done((bf16[112,512]{1,0:T(8,128)(2,1)}, bf16[112,512]{1,0:T(8,128)(2,1)S(1)}, u32[]{:S(2)}, u32[]{:S(2)}) %collective-permute-start) | collective-permute-done | bytes 114720 | tf_op jit(solution)/shard_map/ppermute | solution.py:337
  24.3 2.5 %collective-permute-start.2 = (bf16[56,512]{1,0:T(8,128)(2,1)S(1)}, bf16[56,512]{1,0:T(8,128)(2,1)S(1)}, u32[]{:S(2)}, u32[]{:S(2)}) collective-permute-start(bf16[56,512]{1,0:T(8,128)(2,1)S(1)} %slice.24), channel_id=1, source_target_pairs={{0,3},{1,0},{2,1},{3,2},{4,7},{5,4},{6,5},{7,6},{8,11},{9,8},{10,9... | collective-permute-start | bytes 172040 | tf_op jit(solution)/shard_map/ppermute | solution.py:337
  26.8 0.0 collective-permute-done.4.low
  26.8 0.7 copy-done.21
  27.5 0.7 copy-done.22
  28.3 3.5 %shard_map.121 = (bf16[512,512]{1,0:T(8,128)(2,1)}, f32[512,128]{1,0:T(8,128)}, bf16[768,768]{1,0:T(8,128)(2,1)}) custom-call(bf16[192,768]{1,0:T(8,128)(2,1)} %get-tuple-element.42.own, bf16[192,768]{1,0:T(8,128)(2,1)} %copy-done.21, bf16[192,768]{1,0:T(8,128)(2,1)} %copy-done.20, bf16[192,768]{1,0:T(8,128)(2,1)} %copy-done.22, bf16[768,512]{1,0:T(8,128)(2,1)} %weight.3), custom_call_target="tpu_custom_call" | custom-call | flops 603979776 | bytes 3932160 | tf_op jit(solution)/shard_map/pallas_call | solution.py:30
  31.8 0.6 copy-done.26
  32.3 0.0 copy-done.27
  32.4 15.4 %shard_map.122 = (f32[528,128]{1,0:T(8,128)}, f32[528,128]{1,0:T(8,128)}, f32[528,128]{1,0:T(8,128)}, f32[528,128]{1,0:T(8,128)}, f32[128,512]{1,0:T(8,128)}, /*index=5*/f32[128,512]{1,0:T(8,128)}) custom-call(bf16[112,512]{1,0:T(8,128)(2,1)} %get-tuple-element.41.own, bf16[112,512]{1,0:T(8,128)(2,1)} %copy-done.16, bf16[112,512]{1,0:T(8,128)(2,1)} %copy-done.15, ...), custom_call_target="tpu_custom_call" | custom-call | flops 12000000000 | bytes 2588672 | tf_op jit(solution)/shard_map/pallas_call | solution.py:30
  47.7 0.1 collective-permute-start.9
  47.8 0.1 collective-permute-start.7
  47.9 0.4 collective-permute-start.8
  48.3 1.2 %collective-permute-done.9 = f32[528,128]{1,0:T(8,128)S(1)} collective-permute-done((f32[528,128]{1,0:T(8,128)}, f32[528,128]{1,0:T(8,128)S(1)}, u32[]{:S(2)}, u32[]{:S(2)}) %collective-permute-start.9) | collective-permute-done | bytes 270368 | tf_op jit(solution)/shard_map/ppermute | solution.py:334
  49.6 1.0 add.22
  50.6 1.6 %collective-permute-start.10 = (f32[528,128]{1,0:T(8,128)S(1)}, f32[528,128]{1,0:T(8,128)S(1)}, u32[]{:S(2)}, u32[]{:S(2)}) collective-permute-start(f32[528,128]{1,0:T(8,128)S(1)} %add.22), channel_id=1, source_target_pairs={{0,16},{4,20},{8,24},{12,28},{16,0},{20,4},{24,8},{28,12},{1,17},{... | collective-permute-start | bytes 811016 | tf_op jit(solution)/shard_map/ppermute | solution.py:334
  52.1 4.6 %collective-permute-done.7.recv = f32[128,512]{1,0:T(8,128)S(1)} collective-permute-done((f32[128,512]{1,0:T(8,128)}, f32[128,512]{1,0:T(8,128)S(1)}, u32[]{:S(2)}, u32[]{:S(2)}) %collective-permute-start.7) | collective-permute-done | bytes 262176 | tf_op jit(solution)/shard_map/ppermute | solution.py:340
  56.7 1.0 slice_add_fusion
  57.8 1.0 collective-permute-start.11
  58.8 0.3 collective-permute-done.10.last
  59.1 0.4 copy-done.2
  59.5 0.3 copy-done.3
  59.9 2.9 %shard_map.123 = (f32[400,128]{1,0:T(8,128)}, f32[400,128]{1,0:T(8,128)}, f32[128,128]{1,0:T(8,128)}, f32[128,128]{1,0:T(8,128)}, f32[128,128]{1,0:T(8,128)}, /*index=5*/f32[128,128]{1,0:T(8,128)}) custom-call(f32[528,128]{1,0:T(8,128)} %get-tuple-element.46.keep, f32[528,128]{1,0:T(8,128)} %copy-done.2, f32[528,128]{1,0:T(8,128)} %copy-done.3, ...), custom_call_target="tpu_custom_call" | custom-call | flops 100663296 | bytes 2924544 | tf_op jit(solution)/shard_map/pallas_call | solution.py:30
  62.8 3.7 %collective-permute-done.11.last = f32[64,512]{1,0:T(8,128)S(1)} collective-permute-done((f32[64,512]{1,0:T(8,128)S(1)}, f32[64,512]{1,0:T(8,128)S(1)}, u32[]{:S(2)}, u32[]{:S(2)}) %collective-permute-start.11) | collective-permute-done | bytes 131104 | tf_op jit(solution)/shard_map/ppermute | solution.py:340
  66.5 0.7 copy-done.11
  67.2 1.9 %shard_map.124 = (f32[64,512]{1,0:T(8,128)}, bf16[64,128]{1,0:T(8,128)(2,1)}, bf16[64,128]{1,0:T(8,128)(2,1)}, bf16[64,128]{1,0:T(8,128)(2,1)}, bf16[64,128]{1,0:T(8,128)(2,1)}) custom-call(f32[128,512]{1,0:T(8,128)} %get-tuple-element.44.keep, f32[128,512]{1,0:T(8,128)} %copy-done.1, f32[64,512]{1,0:T(8,128)} %copy-done.11, f32[64,512]{1,0:T(8,128)} %get-tuple-element.55.act), custom_call_target="tpu_custom_call" | custom-call | bytes 983040 | tf_op jit(solution)/shard_map/pallas_call | solution.py:30
  69.0 0.0 collective-permute-start.15
  69.0 1.6 %collective-permute-start.16 = (bf16[64,128]{1,0:T(8,128)(2,1)}, bf16[64,128]{1,0:T(8,128)(2,1)S(1)}, u32[]{:S(2)}, u32[]{:S(2)}) collective-permute-start(bf16[64,128]{1,0:T(8,128)(2,1)} %get-tuple-element.65), channel_id=1, source_target_pairs={{0,16},{4,20},{8,24},{12,28},{16,0},{20,4},{24,8},{28,12},{1,17},{... | collective-permute-start | bytes 49160 | tf_op jit(solution)/shard_map/ppermute | solution.py:334
  70.6 0.3 collective-permute-start.17
  70.9 2.1 %collective-permute-done.16.refs_2_ = bf16[64,128]{1,0:T(8,128)(2,1)S(1)} collective-permute-done((bf16[64,128]{1,0:T(8,128)(2,1)}, bf16[64,128]{1,0:T(8,128)(2,1)S(1)}, u32[]{:S(2)}, u32[]{:S(2)}) %collective-permute-start.16) | collective-permute-done | bytes 16416 | tf_op jit(solution)/shard_map/ppermute | solution.py:334
  73.0 0.9 collective-permute-done.17.refs_3_
  74.0 0.6 copy-done.19
  74.6 2.6 %shard_map.125 = (f32[400,128]{1,0:T(8,128)}, f32[400,128]{1,0:T(8,128)}) custom-call(f32[400,128]{1,0:T(8,128)} %get-tuple-element.61.keep_in, f32[400,128]{1,0:T(8,128)} %get-tuple-element.62.send_in, bf16[768,768]{1,0:T(8,128)(2,1)} %get-tuple-element.51.turned, bf16[64,128]{1,0:T(8,128)(2,1)} %get-tuple-element.63.refs_0_, bf16[64,128]{1,0:T(8,128)(2,1)} %copy-done.17, ...), custom_call_target="tpu_custom_call" | custom-call | flops 50331648 | bytes 2064384 | tf_op jit(solution)/shard_map/pallas_call | solution.py:30
  77.2 1.5 %collective-permute-start.18 = (f32[400,128]{1,0:T(8,128)}, f32[400,128]{1,0:T(8,128)S(1)}, u32[]{:S(2)}, u32[]{:S(2)}) collective-permute-start(f32[400,128]{1,0:T(8,128)} %get-tuple-element.67), channel_id=1, source_target_pairs={{0,8},{4,12},{8,0},{12,4},{16,24},{20,28},{24,16},{28,20},{1,9},{5... | collective-permute-start | bytes 614408 | tf_op jit(solution)/shard_map/ppermute | solution.py:334
  78.7 0.7 collective-permute-start.13
  79.4 1.1 collective-permute-start.14
  80.5 3.2 %collective-permute-done.13.refs_2_ = f32[128,128]{1,0:T(8,128)S(1)} collective-permute-done((f32[128,128]{1,0:T(8,128)S(1)}, f32[128,128]{1,0:T(8,128)S(1)}, u32[]{:S(2)}, u32[]{:S(2)}) %collective-permute-start.13) | collective-permute-done | bytes 65568 | tf_op jit(solution)/shard_map/ppermute | solution.py:334
  83.7 0.3 collective-permute-done.14.refs_3_
  84.0 0.5 collective-permute-done.18
  84.5 1.0 add.24
  85.5 0.1 collective-permute-start.19
  85.6 1.7 %shard_map.126 = f32[128,512]{1,0:T(8,128)} custom-call(f32[128,128]{1,0:T(8,128)} %get-tuple-element.68.refs_0_, f32[128,128]{1,0:T(8,128)} %copy-done.12, f32[128,128]{1,0:T(8,128)} %copy-done.13, f32[128,128]{1,0:T(8,128)} %copy-done.14), custom_call_target="tpu_custom_call" | custom-call | bytes 524288 | tf_op jit(solution)/shard_map/pallas_call | solution.py:30
  87.3 5.4 %collective-permute-done.19 = f32[400,128]{1,0:T(8,128)S(1)} collective-permute-done((f32[400,128]{1,0:T(8,128)S(1)}, f32[400,128]{1,0:T(8,128)S(1)}, u32[]{:S(2)}, u32[]{:S(2)}) %collective-permute-start.19) | collective-permute-done | bytes 204832 | tf_op jit(solution)/shard_map/ppermute | solution.py:340
  92.7 2.0 %collective-permute-start.20 = (f32[400,128]{1,0:T(8,128)S(1)}, f32[400,128]{1,0:T(8,128)S(1)}, u32[]{:S(2)}, u32[]{:S(2)}) collective-permute-start(f32[400,128]{1,0:T(8,128)S(1)} %add.25), channel_id=1, source_target_pairs={{0,3},{1,2},{2,1},{3,0},{4,7},{5,6},{6,5},{7,4},{8,11},{9,10},{10,... | collective-permute-start | bytes 614408 | tf_op jit(solution)/shard_map/ppermute | solution.py:340
  94.7 6.3 %collective-permute-done.20 = f32[400,128]{1,0:T(8,128)S(1)} collective-permute-done((f32[400,128]{1,0:T(8,128)S(1)}, f32[400,128]{1,0:T(8,128)S(1)}, u32[]{:S(2)}, u32[]{:S(2)}) %collective-permute-start.20) | collective-permute-done | bytes 204832 | tf_op jit(solution)/shard_map/ppermute | solution.py:340
  101.0 0.2 collective-permute-start.26
  101.1 2.0 %collective-permute-start.24 = (f32[400,128]{1,0:T(8,128)S(1)}, f32[400,128]{1,0:T(8,128)S(1)}, u32[]{:S(2)}, u32[]{:S(2)}) collective-permute-start(f32[400,128]{1,0:T(8,128)S(1)} %add.26.refs_0_), channel_id=1, source_target_pairs={{0,8},{4,12},{8,0},{12,4},{16,24},{20,28},{24,16},{28,20},{1,9},{5... | collective-permute-start | bytes 614408 | tf_op jit(solution)/shard_map/ppermute | solution.py:334
  103.1 1.4 %collective-permute-start.22 = (f32[400,128]{1,0:T(8,128)S(1)}, f32[400,128]{1,0:T(8,128)S(1)}, u32[]{:S(2)}, u32[]{:S(2)}) collective-permute-start(f32[400,128]{1,0:T(8,128)S(1)} %add.26.refs_0_), channel_id=1, source_target_pairs={{0,16},{4,20},{8,24},{12,28},{16,0},{20,4},{24,8},{28,12},{1,17},{... | collective-permute-start | bytes 614408 | tf_op jit(solution)/shard_map/ppermute | solution.py:334
  104.5 5.0 %collective-permute-done.26.refs_6_ = f32[400,128]{1,0:T(8,128)S(1)} collective-permute-done((f32[400,128]{1,0:T(8,128)S(1)}, f32[400,128]{1,0:T(8,128)S(1)}, u32[]{:S(2)}, u32[]{:S(2)}) %collective-permute-start.26) | collective-permute-done | bytes 204832 | tf_op jit(solution)/shard_map/ppermute | solution.py:334
  109.5 1.3 %collective-permute-done.24.refs_4_ = f32[400,128]{1,0:T(8,128)S(1)} collective-permute-done((f32[400,128]{1,0:T(8,128)S(1)}, f32[400,128]{1,0:T(8,128)S(1)}, u32[]{:S(2)}, u32[]{:S(2)}) %collective-permute-start.24) | collective-permute-done | bytes 204832 | tf_op jit(solution)/shard_map/ppermute | solution.py:334
  110.9 0.8 collective-permute-done.22.refs_2_
  111.8 0.6 collective-permute-done.25.refs_5_
  112.3 0.8 collective-permute-done.23.refs_3_
  113.2 0.7 copy-done.10
  113.9 2.8 %shard_map.127 = (f32[768,512]{1,0:T(8,128)}, f32[3,512]{1,0:T(4,128)}) custom-call(f32[400,128]{1,0:T(8,128)} %copy-done, f32[400,128]{1,0:T(8,128)} %copy-done.7, f32[400,128]{1,0:T(8,128)} %copy-done.6, f32[400,128]{1,0:T(8,128)} %copy-done.10, f32[400,128]{1,0:T(8,128)} %copy-done.5, f32[400,128]{1,0:T(8,128)} %copy-done.9, f32[400,128]{1,0:T(8,128)} %copy-done.4, ...), custom_call_target="tpu_custom_call" | custom-call | bytes 3217408 | tf_op jit(solution)/shard_map/pallas_call | solution.py:30
  (64 shorter events, 0.2 us)
Async XLA Ops:
  4.4 10.2 %collective-permute-start.5 = (bf16[192,768]{1,0:T(8,128)(2,1)}, bf16[192,768]{1,0:T(8,128)(2,1)S(1)}, u32[]{:S(2)}, u32[]{:S(2)}) collective-permute-start(bf16[192,768]{1,0:T(8,128)(2,1)} %get-tuple-element.42.own), channel_id=1, source_target_pairs={{0,16},{4,20},{8,24},{12,28},{16,0},{20,4},{24,8},{28,12},{1,17},{... | collective-permute-start | bytes 884744 | tf_op jit(solution)/shard_map/ppermute | solution.py:334
  7.4 19.4 %collective-permute-start.4 = (bf16[192,768]{1,0:T(8,128)(2,1)}, bf16[192,768]{1,0:T(8,128)(2,1)S(1)}, u32[]{:S(2)}, u32[]{:S(2)}) collective-permute-start(bf16[192,768]{1,0:T(8,128)(2,1)} %get-tuple-element.42.own), channel_id=1, source_target_pairs={{0,4},{4,0},{8,12},{12,8},{16,20},{20,16},{24,28},{28,24},{1,5},{5... | collective-permute-start | bytes 884744 | tf_op jit(solution)/shard_map/ppermute | solution.py:334
  14.6 12.2 %copy-start.20 = (bf16[192,768]{1,0:T(8,128)(2,1)}, bf16[192,768]{1,0:T(8,128)(2,1)S(1)}, u32[]{:S(2)}) copy-start(bf16[192,768]{1,0:T(8,128)(2,1)S(1)} %collective-permute-done.5.high) | copy-start | bytes 884740
  14.6 12.2 %collective-permute-start.6 = (bf16[192,768]{1,0:T(8,128)(2,1)S(1)}, bf16[192,768]{1,0:T(8,128)(2,1)S(1)}, u32[]{:S(2)}, u32[]{:S(2)}) collective-permute-start(bf16[192,768]{1,0:T(8,128)(2,1)S(1)} %collective-permute-done.5.high), channel_id=1, source_target_pairs={{0,4},{4,0},{8,12},{12,8},{16,20},{20,16},{24,28},{28,24},{1,5},{5... | collective-permute-start | bytes 884744 | tf_op jit(solution)/shard_map/ppermute | solution.py:334
  14.6 8.1 %collective-permute-start.1 = (bf16[112,512]{1,0:T(8,128)(2,1)}, bf16[112,512]{1,0:T(8,128)(2,1)S(1)}, u32[]{:S(2)}, u32[]{:S(2)}) collective-permute-start(bf16[112,512]{1,0:T(8,128)(2,1)} %get-tuple-element.41.own), channel_id=1, source_target_pairs={{0,1},{1,2},{2,3},{3,0},{4,5},{5,6},{6,7},{7,4},{8,9},{9,10},{10,1... | collective-permute-start | bytes 344072 | tf_op jit(solution)/shard_map/ppermute | solution.py:337
  16.4 7.9 %collective-permute-start = (bf16[112,512]{1,0:T(8,128)(2,1)}, bf16[112,512]{1,0:T(8,128)(2,1)S(1)}, u32[]{:S(2)}, u32[]{:S(2)}) collective-permute-start(bf16[112,512]{1,0:T(8,128)(2,1)} %get-tuple-element.41.own), channel_id=1, source_target_pairs={{0,3},{1,0},{2,1},{3,2},{4,7},{5,4},{6,5},{7,6},{8,11},{9,8},{10,9... | collective-permute-start | bytes 344072 | tf_op jit(solution)/shard_map/ppermute | solution.py:337
  22.7 9.1 %copy-start.15 = (bf16[112,512]{1,0:T(8,128)(2,1)}, bf16[112,512]{1,0:T(8,128)(2,1)S(1)}, u32[]{:S(2)}) copy-start(bf16[112,512]{1,0:T(8,128)(2,1)S(1)} %collective-permute-done.1.minus) | copy-start | bytes 344068
  22.7 9.1 %collective-permute-start.3 = (bf16[56,512]{1,0:T(8,128)(2,1)S(1)}, bf16[56,512]{1,0:T(8,128)(2,1)S(1)}, u32[]{:S(2)}, u32[]{:S(2)}) collective-permute-start(bf16[56,512]{1,0:T(8,128)(2,1)S(1)} %slice.25), channel_id=1, source_target_pairs={{0,1},{1,2},{2,3},{3,0},{4,5},{5,6},{6,7},{7,4},{8,9},{9,10},{10,1... | collective-permute-start | bytes 172040 | tf_op jit(solution)/shard_map/ppermute | solution.py:337
  24.3 7.4 %copy-start.16 = (bf16[112,512]{1,0:T(8,128)(2,1)}, bf16[112,512]{1,0:T(8,128)(2,1)S(1)}, u32[]{:S(2)}) copy-start(bf16[112,512]{1,0:T(8,128)(2,1)S(1)} %collective-permute-done.plus) | copy-start | bytes 344068
  24.3 7.4 %collective-permute-start.2 = (bf16[56,512]{1,0:T(8,128)(2,1)S(1)}, bf16[56,512]{1,0:T(8,128)(2,1)S(1)}, u32[]{:S(2)}, u32[]{:S(2)}) collective-permute-start(bf16[56,512]{1,0:T(8,128)(2,1)S(1)} %slice.24), channel_id=1, source_target_pairs={{0,3},{1,0},{2,1},{3,2},{4,7},{5,4},{6,5},{7,6},{8,11},{9,8},{10,9... | collective-permute-start | bytes 172040 | tf_op jit(solution)/shard_map/ppermute | solution.py:337
  26.8 0.7 copy-start.21
  27.5 0.7 copy-start.22
  31.7 0.6 copy-start.26
  31.7 0.6 copy-start.27
  47.7 1.8 %collective-permute-start.9 = (f32[528,128]{1,0:T(8,128)}, f32[528,128]{1,0:T(8,128)S(1)}, u32[]{:S(2)}, u32[]{:S(2)}) collective-permute-start(f32[528,128]{1,0:T(8,128)} %get-tuple-element.49), channel_id=1, source_target_pairs={{0,4},{4,0},{8,12},{12,8},{16,20},{20,16},{24,28},{28,24},{1,5},{5... | collective-permute-start | bytes 811016 | tf_op jit(solution)/shard_map/ppermute | solution.py:334
  47.8 8.9 %collective-permute-start.7 = (f32[128,512]{1,0:T(8,128)}, f32[128,512]{1,0:T(8,128)S(1)}, u32[]{:S(2)}, u32[]{:S(2)}) collective-permute-start(f32[128,512]{1,0:T(8,128)} %get-tuple-element.45), channel_id=1, source_target_pairs={{0,1},{1,0},{2,3},{3,2},{4,5},{5,4},{6,7},{7,6},{8,9},{9,8},{10,11... | collective-permute-start | bytes 786440 | tf_op jit(solution)/shard_map/ppermute | solution.py:340
  47.9 10.9 %collective-permute-start.8 = (f32[528,128]{1,0:T(8,128)}, f32[528,128]{1,0:T(8,128)S(1)}, u32[]{:S(2)}, u32[]{:S(2)}) collective-permute-start(f32[528,128]{1,0:T(8,128)} %get-tuple-element.47), channel_id=1, source_target_pairs={{0,4},{4,0},{8,12},{12,8},{16,20},{20,16},{24,28},{28,24},{1,5},{5... | collective-permute-start | bytes 811016 | tf_op jit(solution)/shard_map/ppermute | solution.py:334
  50.6 8.6 %collective-permute-start.10 = (f32[528,128]{1,0:T(8,128)S(1)}, f32[528,128]{1,0:T(8,128)S(1)}, u32[]{:S(2)}, u32[]{:S(2)}) collective-permute-start(f32[528,128]{1,0:T(8,128)S(1)} %add.22), channel_id=1, source_target_pairs={{0,16},{4,20},{8,24},{12,28},{16,0},{20,4},{24,8},{28,12},{1,17},{... | collective-permute-start | bytes 811016 | tf_op jit(solution)/shard_map/ppermute | solution.py:334
  56.7 9.8 %copy-start.1 = (f32[128,512]{1,0:T(8,128)}, f32[128,512]{1,0:T(8,128)S(1)}, u32[]{:S(2)}) copy-start(f32[128,512]{1,0:T(8,128)S(1)} %collective-permute-done.7.recv) | copy-start | bytes 786436
  57.8 8.7 %collective-permute-start.11 = (f32[64,512]{1,0:T(8,128)S(1)}, f32[64,512]{1,0:T(8,128)S(1)}, u32[]{:S(2)}, u32[]{:S(2)}) collective-permute-start(f32[64,512]{1,0:T(8,128)S(1)} %slice_add_fusion), channel_id=1, source_target_pairs={{0,2},{1,3},{2,0},{3,1},{4,6},{5,7},{6,4},{7,5},{8,10},{9,11},{10,... | collective-permute-start | bytes 393224 | tf_op jit(solution)/shard_map/ppermute | solution.py:340
  58.8 0.7 copy-start.2
  59.1 0.7 copy-start.3
  62.8 15.9 %copy-start.25 = (f32[128,128]{1,0:T(8,128)S(1)}, f32[128,128]{1,0:T(8,128)}, u32[]{:S(2)}) copy-start(f32[128,128]{1,0:T(8,128)} %get-tuple-element.58) | copy-start | bytes 196612
  62.8 15.9 %copy-start.24 = (f32[128,128]{1,0:T(8,128)S(1)}, f32[128,128]{1,0:T(8,128)}, u32[]{:S(2)}) copy-start(f32[128,128]{1,0:T(8,128)} %get-tuple-element.59) | copy-start | bytes 196612
  62.8 16.6 %copy-start.23 = (f32[128,128]{1,0:T(8,128)S(1)}, f32[128,128]{1,0:T(8,128)}, u32[]{:S(2)}) copy-start(f32[128,128]{1,0:T(8,128)} %get-tuple-element.60) | copy-start | bytes 196612
  66.5 0.7 copy-start.11
  69.0 1.9 %collective-permute-start.15 = (bf16[64,128]{1,0:T(8,128)(2,1)}, bf16[64,128]{1,0:T(8,128)(2,1)S(1)}, u32[]{:S(2)}, u32[]{:S(2)}) collective-permute-start(bf16[64,128]{1,0:T(8,128)(2,1)} %get-tuple-element.64), channel_id=1, source_target_pairs={{0,4},{4,0},{8,12},{12,8},{16,20},{20,16},{24,28},{28,24},{1,5},{5... | collective-permute-start | bytes 49160 | tf_op jit(solution)/shard_map/ppermute | solution.py:334
  69.0 4.0 %collective-permute-start.16 = (bf16[64,128]{1,0:T(8,128)(2,1)}, bf16[64,128]{1,0:T(8,128)(2,1)S(1)}, u32[]{:S(2)}, u32[]{:S(2)}) collective-permute-start(bf16[64,128]{1,0:T(8,128)(2,1)} %get-tuple-element.65), channel_id=1, source_target_pairs={{0,16},{4,20},{8,24},{12,28},{16,0},{20,4},{24,8},{28,12},{1,17},{... | collective-permute-start | bytes 49160 | tf_op jit(solution)/shard_map/ppermute | solution.py:334
  70.6 3.4 %collective-permute-start.17 = (bf16[64,128]{1,0:T(8,128)(2,1)}, bf16[64,128]{1,0:T(8,128)(2,1)S(1)}, u32[]{:S(2)}, u32[]{:S(2)}) collective-permute-start(bf16[64,128]{1,0:T(8,128)(2,1)} %get-tuple-element.66), channel_id=1, source_target_pairs={{0,20},{4,16},{8,28},{12,24},{16,4},{20,0},{24,12},{28,8},{1,21},{... | collective-permute-start | bytes 49160 | tf_op jit(solution)/shard_map/ppermute | solution.py:334
  70.9 3.1 %copy-start.17 = (bf16[64,128]{1,0:T(8,128)(2,1)}, bf16[64,128]{1,0:T(8,128)(2,1)S(1)}, u32[]{:S(2)}) copy-start(bf16[64,128]{1,0:T(8,128)(2,1)S(1)} %collective-permute-done.15.refs_1_) | copy-start | bytes 49156
  73.0 1.0 copy-start.18
  74.0 0.6 copy-start.19
  77.2 7.4 %collective-permute-start.18 = (f32[400,128]{1,0:T(8,128)}, f32[400,128]{1,0:T(8,128)S(1)}, u32[]{:S(2)}, u32[]{:S(2)}) collective-permute-start(f32[400,128]{1,0:T(8,128)} %get-tuple-element.67), channel_id=1, source_target_pairs={{0,8},{4,12},{8,0},{12,4},{16,24},{20,28},{24,16},{28,20},{1,9},{5... | collective-permute-start | bytes 614408 | tf_op jit(solution)/shard_map/ppermute | solution.py:334
  78.7 1.9 %collective-permute-start.12 = (f32[128,128]{1,0:T(8,128)S(1)}, f32[128,128]{1,0:T(8,128)S(1)}, u32[]{:S(2)}, u32[]{:S(2)}) collective-permute-start(f32[128,128]{1,0:T(8,128)S(1)} %copy-done.25), channel_id=1, source_target_pairs={{0,4},{4,0},{8,12},{12,8},{16,20},{20,16},{24,28},{28,24},{1,5},{5... | collective-permute-start | bytes 196616 | tf_op jit(solution)/shard_map/ppermute | solution.py:334
  78.7 5.0 %collective-permute-start.13 = (f32[128,128]{1,0:T(8,128)S(1)}, f32[128,128]{1,0:T(8,128)S(1)}, u32[]{:S(2)}, u32[]{:S(2)}) collective-permute-start(f32[128,128]{1,0:T(8,128)S(1)} %copy-done.24), channel_id=1, source_target_pairs={{0,16},{4,20},{8,24},{12,28},{16,0},{20,4},{24,8},{28,12},{1,17},{... | collective-permute-start | bytes 196616 | tf_op jit(solution)/shard_map/ppermute | solution.py:334
  79.4 4.6 %collective-permute-start.14 = (f32[128,128]{1,0:T(8,128)S(1)}, f32[128,128]{1,0:T(8,128)S(1)}, u32[]{:S(2)}, u32[]{:S(2)}) collective-permute-start(f32[128,128]{1,0:T(8,128)S(1)} %copy-done.23), channel_id=1, source_target_pairs={{0,20},{4,16},{8,28},{12,24},{16,4},{20,0},{24,12},{28,8},{1,21},{... | collective-permute-start | bytes 196616 | tf_op jit(solution)/shard_map/ppermute | solution.py:334
  80.5 5.0 %copy-start.12 = (f32[128,128]{1,0:T(8,128)}, f32[128,128]{1,0:T(8,128)S(1)}, u32[]{:S(2)}) copy-start(f32[128,128]{1,0:T(8,128)S(1)} %collective-permute-done.12.refs_1_) | copy-start | bytes 196612
  83.7 1.9 %copy-start.13 = (f32[128,128]{1,0:T(8,128)}, f32[128,128]{1,0:T(8,128)S(1)}, u32[]{:S(2)}) copy-start(f32[128,128]{1,0:T(8,128)S(1)} %collective-permute-done.13.refs_2_) | copy-start | bytes 196612
  84.0 1.5 %copy-start.14 = (f32[128,128]{1,0:T(8,128)}, f32[128,128]{1,0:T(8,128)S(1)}, u32[]{:S(2)}) copy-start(f32[128,128]{1,0:T(8,128)S(1)} %collective-permute-done.14.refs_3_) | copy-start | bytes 196612
  85.5 7.2 %collective-permute-start.19 = (f32[400,128]{1,0:T(8,128)S(1)}, f32[400,128]{1,0:T(8,128)S(1)}, u32[]{:S(2)}, u32[]{:S(2)}) collective-permute-start(f32[400,128]{1,0:T(8,128)S(1)} %add.24), channel_id=1, source_target_pairs={{0,1},{1,0},{2,3},{3,2},{4,5},{5,4},{6,7},{7,6},{8,9},{9,8},{10,11... | collective-permute-start | bytes 614408 | tf_op jit(solution)/shard_map/ppermute | solution.py:340
  92.7 8.2 %collective-permute-start.20 = (f32[400,128]{1,0:T(8,128)S(1)}, f32[400,128]{1,0:T(8,128)S(1)}, u32[]{:S(2)}, u32[]{:S(2)}) collective-permute-start(f32[400,128]{1,0:T(8,128)S(1)} %add.25), channel_id=1, source_target_pairs={{0,3},{1,2},{2,1},{3,0},{4,7},{5,6},{6,5},{7,4},{8,11},{9,10},{10,... | collective-permute-start | bytes 614408 | tf_op jit(solution)/shard_map/ppermute | solution.py:340
  101.0 12.2 %copy-start = (f32[400,128]{1,0:T(8,128)}, f32[400,128]{1,0:T(8,128)S(1)}, u32[]{:S(2)}) copy-start(f32[400,128]{1,0:T(8,128)S(1)} %add.26.refs_0_) | copy-start | bytes 614404
  101.0 8.6 %collective-permute-start.26 = (f32[400,128]{1,0:T(8,128)S(1)}, f32[400,128]{1,0:T(8,128)S(1)}, u32[]{:S(2)}, u32[]{:S(2)}) collective-permute-start(f32[400,128]{1,0:T(8,128)S(1)} %add.26.refs_0_), channel_id=1, source_target_pairs={{0,24},{4,28},{8,16},{12,20},{16,8},{20,12},{24,0},{28,4},{1,25},{... | collective-permute-start | bytes 614408 | tf_op jit(solution)/shard_map/ppermute | solution.py:334
  101.1 9.7 %collective-permute-start.24 = (f32[400,128]{1,0:T(8,128)S(1)}, f32[400,128]{1,0:T(8,128)S(1)}, u32[]{:S(2)}, u32[]{:S(2)}) collective-permute-start(f32[400,128]{1,0:T(8,128)S(1)} %add.26.refs_0_), channel_id=1, source_target_pairs={{0,8},{4,12},{8,0},{12,4},{16,24},{20,28},{24,16},{28,20},{1,9},{5... | collective-permute-start | bytes 614408 | tf_op jit(solution)/shard_map/ppermute | solution.py:334
  103.1 8.6 %collective-permute-start.22 = (f32[400,128]{1,0:T(8,128)S(1)}, f32[400,128]{1,0:T(8,128)S(1)}, u32[]{:S(2)}, u32[]{:S(2)}) collective-permute-start(f32[400,128]{1,0:T(8,128)S(1)} %add.26.refs_0_), channel_id=1, source_target_pairs={{0,16},{4,20},{8,24},{12,28},{16,0},{20,4},{24,8},{28,12},{1,17},{... | collective-permute-start | bytes 614408 | tf_op jit(solution)/shard_map/ppermute | solution.py:334
  104.5 7.2 %collective-permute-start.21 = (f32[400,128]{1,0:T(8,128)S(1)}, f32[400,128]{1,0:T(8,128)S(1)}, u32[]{:S(2)}, u32[]{:S(2)}) collective-permute-start(f32[400,128]{1,0:T(8,128)S(1)} %add.26.refs_0_), channel_id=1, source_target_pairs={{0,4},{4,0},{8,12},{12,8},{16,20},{20,16},{24,28},{28,24},{1,5},{5... | collective-permute-start | bytes 614408 | tf_op jit(solution)/shard_map/ppermute | solution.py:334
  109.5 3.6 %copy-start.4 = (f32[400,128]{1,0:T(8,128)}, f32[400,128]{1,0:T(8,128)S(1)}, u32[]{:S(2)}) copy-start(f32[400,128]{1,0:T(8,128)S(1)} %collective-permute-done.26.refs_6_) | copy-start | bytes 614404
  109.5 2.2 %collective-permute-start.27 = (f32[400,128]{1,0:T(8,128)S(1)}, f32[400,128]{1,0:T(8,128)S(1)}, u32[]{:S(2)}, u32[]{:S(2)}) collective-permute-start(f32[400,128]{1,0:T(8,128)S(1)} %collective-permute-done.26.refs_6_), channel_id=1, source_target_pairs={{0,4},{4,0},{8,12},{12,8},{16,20},{20,16},{24,28},{28,24},{1,5},{5... | collective-permute-start | bytes 614408 | tf_op jit(solution)/shard_map/ppermute | solution.py:334
  110.9 2.3 %copy-start.5 = (f32[400,128]{1,0:T(8,128)}, f32[400,128]{1,0:T(8,128)S(1)}, u32[]{:S(2)}) copy-start(f32[400,128]{1,0:T(8,128)S(1)} %collective-permute-done.24.refs_4_) | copy-start | bytes 614404
  110.9 1.5 %collective-permute-start.25 = (f32[400,128]{1,0:T(8,128)S(1)}, f32[400,128]{1,0:T(8,128)S(1)}, u32[]{:S(2)}, u32[]{:S(2)}) collective-permute-start(f32[400,128]{1,0:T(8,128)S(1)} %collective-permute-done.24.refs_4_), channel_id=1, source_target_pairs={{0,4},{4,0},{8,12},{12,8},{16,20},{20,16},{24,28},{28,24},{1,5},{5... | collective-permute-start | bytes 614408 | tf_op jit(solution)/shard_map/ppermute | solution.py:334
  111.7 1.5 %copy-start.6 = (f32[400,128]{1,0:T(8,128)}, f32[400,128]{1,0:T(8,128)S(1)}, u32[]{:S(2)}) copy-start(f32[400,128]{1,0:T(8,128)S(1)} %collective-permute-done.22.refs_2_) | copy-start | bytes 614404
  111.7 1.5 %collective-permute-start.23 = (f32[400,128]{1,0:T(8,128)S(1)}, f32[400,128]{1,0:T(8,128)S(1)}, u32[]{:S(2)}, u32[]{:S(2)}) collective-permute-start(f32[400,128]{1,0:T(8,128)S(1)} %collective-permute-done.22.refs_2_), channel_id=1, source_target_pairs={{0,4},{4,0},{8,12},{12,8},{16,20},{20,16},{24,28},{28,24},{1,5},{5... | collective-permute-start | bytes 614408 | tf_op jit(solution)/shard_map/ppermute | solution.py:334
  111.7 1.5 %copy-start.7 = (f32[400,128]{1,0:T(8,128)}, f32[400,128]{1,0:T(8,128)S(1)}, u32[]{:S(2)}) copy-start(f32[400,128]{1,0:T(8,128)S(1)} %collective-permute-done.21.refs_1_) | copy-start | bytes 614404
  111.8 1.5 %copy-start.8 = (f32[400,128]{1,0:T(8,128)}, f32[400,128]{1,0:T(8,128)S(1)}, u32[]{:S(2)}) copy-start(f32[400,128]{1,0:T(8,128)S(1)} %collective-permute-done.27.refs_7_) | copy-start | bytes 614404
  112.3 0.9 copy-start.9
  113.2 0.7 copy-start.10
where the time goes:
time: 118 us; the launch traced here: 117 us
  waiting for transfers between devices  50.3 us (43%)
  Pallas kernels  33.1 us (28%)
  starting transfers between devices  23.4 us (20%)
  local copies, waits for them, and re-layouts  4.78 us (4%)
  other arithmetic  4.34 us (4%)
    pallas_call x8, Pallas kernels, call(): pl.pallas_call(body, out_shape=tuple(outs), in_specs=in_specs or [VMEM] *...  33.1 us
    ppermute x20, waiting for transfers between devices, met(): return lax.ppermute(x, 'bucket', [(i, i ^ mask) for i in range(buckets)])  24.5 us
    ppermute x4, waiting for transfers between devices, crossed(): return lax.ppermute(x, 'rel', [(i, i ^ mask) for i in range(groups)])  20 us
    ppermute x20, starting transfers between devices, met(): return lax.ppermute(x, 'bucket', [(i, i ^ mask) for i in range(buckets)])  13.9 us
    ppermute x4, starting transfers between devices, ring(): lax.ppermute(x, 'rel', [(i, (i - step) % groups) for i in range(groups)])  6.39 us
    ppermute x4, waiting for transfers between devices, ring(): lax.ppermute(x, 'rel', [(i, (i - step) % groups) for i in range(groups)])  5.8 us
    unnamed x56, local copies, waits for them, and re-layouts  4.77 us
    ppermute x4, starting transfers between devices, crossed(): return lax.ppermute(x, 'rel', [(i, i ^ mask) for i in range(groups)])  3.13 us
  transfers between devices with their start and end apart: 28, of which 19 were waited for; matrix products, arithmetic and copies ran while one was open for 2% of the time, Pallas kernels for 7%

commit v1 on v0

--- a/solution.py
+++ b/solution.py
@@ -8,6 +8,7 @@
 from jax.sharding import PartitionSpec as P
 
 
+CHUNKS = 2
 LABELLED = 1024.0
 LOG2E = 1.4426950408889634
 SLOT_OF = (0, 1, 3, 2)
@@ -79,7 +80,7 @@
                 done += n
 
 
-def first_body(fields, rows, src_feat, tgt_feat, weight, src, tgt, rel, neg, lab, shift, out, act, feats, flat):
+def first_body(fields, rows, src_feat, weight, src, tgt, rel, neg, lab, shift, out, act, flat):
     pack(fields, rows, src, tgt, rel, neg, lab, flat)
     n = src_feat.shape[0]
     value = jnp.tanh(dot(src_feat[...], weight[...], NN))
@@ -89,8 +90,6 @@
     out[n : n + tasks, :] = flat[...].astype(BF16)
     out[n + tasks :, :] = jnp.zeros_like(out[n + tasks :, :])
     out[n + tasks : n + tasks + shift.shape[0], :] = shift[...]
-    feats[:n, :] = src_feat[...]
-    feats[n:, :] = tgt_feat[...]
 
 
 def take(block, fields, key):
@@ -134,16 +133,21 @@
     return pl.ds(pl.multiple_of(base + number * size, size), size)
 
 
-def prepare_body(size, s_rows, own, low, high, far, weight, emb, act, turned, held):
-    t_rows = own.shape[0] - s_rows
-    me = own_quarter(size)
+def encode_body(own, low, high, far, weight, emb, held):
+    n = own.shape[0]
     for j, x in enumerate((own, low, high, far)):
-        held[aligned(me ^ APART[j], s_rows), :] = x[:s_rows, :]
-        held[pl.ds(pl.multiple_of(4 * s_rows + (me ^ APART[j]) * t_rows, s_rows), t_rows), :] = x[s_rows:, :]
-        emb[j * t_rows : (j + 1) * t_rows, :] = jnp.tanh(dot(x[s_rows:, :], weight[...], NN)).astype(BF16)
-    columns = weight[:, aligned(me, act.shape[1])]
-    act[...] = jnp.tanh(dot(held[4 * s_rows :, :], columns, NN))
-    turned[...] = held[...].astype(F32).T.astype(BF16)
+        held[j * n : (j + 1) * n, :] = x[...]
+    emb[...] = jnp.tanh(dot(held[...], weight[...], NN)).astype(BF16)
+
+
+def prepare_body(size, *refs):
+    src, tgt, weight, (act, src_turned, tgt_turned, src_held, tgt_held) = refs[:4], refs[4:8], refs[8], refs[9:]
+    me = own_quarter(size)
+    for feats, held, turned in ((src, src_held, src_turned), (tgt, tgt_held, tgt_turned)):
+        for j, x in enumerate(feats):
+            held[aligned(me ^ APART[j], x.shape[0]), :] = x[...]
+        turned[...] = held[...].astype(F32).T.astype(BF16)
+    act[...] = jnp.tanh(dot(tgt_held[...], weight[:, aligned(me, act.shape[1])], NN))
 
 
 def start_all(copies, sems):
@@ -176,8 +180,8 @@
 
 def meets_body(cfg, own, plus, minus, far_a, far_b, tgt, *refs):
     fields, rows, s_rows, t_rows, n_rel, scale, groups, negs, size = cfg
-    t_outs, s_keep, s_send = refs[:4], refs[4], refs[5]
-    src, idx, query, parts, acc, w_src, w_rel, total, sems = refs[6:]
+    t_outs, s_outs = refs[:4], refs[4:8]
+    src, idx, query_a, query_b, parts_a, parts_b, acc, w_src, w_rel, total, sems = refs[8:]
     ring = lax.axis_index("rel")
     tasks = idx.shape[1] - 16
 
@@ -185,7 +189,7 @@
         return (0, s_rows, src.at[pl.ds(place * s_rows, s_rows)]), (s_rows, own.shape[0], idx.at[place])
 
     start_all(spread((own, plus, minus, far_a, far_b), places), sems)
-    for ref in (acc, w_src, w_rel):
+    for ref in (acc, w_src, w_rel, query_b, parts_b):
         ref[...] = jnp.zeros_like(ref)
     all_src = src.shape[0]
     all_tgt = t_rows * groups
@@ -193,7 +197,7 @@
     tgt_base = (ring * t_rows).astype(F32)
     lane = lax.broadcasted_iota(jnp.int32, (t_rows, w_rel.shape[1]), 1)
 
-    def step(group, carry):
+    def one_group(group, query, parts):
         shift = idx[group, tasks : tasks + 16, :]
         place = lax.rem(group + ring, groups) * n_rel
         for k in range(n_rel):
@@ -226,18 +230,23 @@
                 line = jnp.where(lane == place + k, jnp.sum(value, axis=1, keepdims=True), line)
             w_src[mine, :] += part
             w_rel[mine, :] += line
-        acc[...] += dot(parts[...], query[...], NN)
+
+    def step(pair, carry):
+        one_group(2 * pair, query_a, parts_a)
+        acc[...] += dot(parts_b[...], query_b[...], NN)
+        one_group(2 * pair + 1, query_b, parts_b)
+        acc[...] += dot(parts_a[...], query_a[...], NN)
         return carry
 
-    lax.fori_loop(0, groups, step, 0)
+    lax.fori_loop(0, groups // 2, step, 0)
+    acc[...] += dot(parts_b[...], query_b[...], NN)
     whole = jnp.concatenate([w_src[...].T, w_rel[...].T[:16, :]], axis=0)
     high = whole.astype(BF16)
     low = (whole - high.astype(F32)).astype(BF16)
     total[...] = scale * (dot(high, tgt[...], NN) + dot(low, tgt[...], NN))
-    for r in range(groups):
-        out = s_send if r % 2 else s_keep
+    for r, out in enumerate(s_outs):
         place = lax.rem((ring ^ r) - ring + groups, groups)
-        out[(r // 2) * s_rows : (r // 2 + 1) * s_rows, :] = total[aligned(place, s_rows), :]
+        out[...] = total[aligned(place, s_rows), :]
     me = own_quarter(size)
     for i, out in enumerate(t_outs):
         lanes = aligned(me ^ APART[i], out.shape[1])
@@ -247,9 +256,8 @@
         out[4 * t_rows :, :] = total[all_src:, lanes]
 
 
-def source_body(size, keep, recv, last, act, grad, *outs):
-    n = grad.shape[0]
-    value = (keep[:n, :] + recv[:n, :]) + last[...]
+def source_body(size, a, b, c, d, act, grad, *outs):
+    value = (a[...] + b[...]) + (c[...] + d[...])
     grad[...] = value
     d = (value * (1.0 - act[...] * act[...])).astype(BF16)
     wide = outs[0].shape[1]
@@ -268,9 +276,8 @@
     n = act.shape[0]
     d = (value[:n, :] * (1.0 - act[...] * act[...])).astype(BF16)
     block = turned.shape[0] // 2
-    first = turned.shape[1] - n
     for r, out in enumerate(parts):
-        out[:block, :] = dot(turned[aligned(own_half() ^ r, block), first:], d, NN)
+        out[:block, :] = dot(turned[aligned(own_half() ^ r, block), :], d, NN)
         out[block:, :] = value[n:, :]
     me = own_quarter(size)
     for a in range(4):
@@ -282,15 +289,19 @@
 
 
 def join_body(size, keep_in, send_in, turned, *refs):
-    pieces, (keep, send), held = refs[:4], refs[4:6], refs[6]
+    pieces, outs, held = refs[:4], refs[4:-1], refs[-1]
     n = pieces[0].shape[0]
     me = own_quarter(size)
     for j, x in enumerate(pieces):
         held[aligned(me ^ APART[j], n), :] = x[...]
     block = turned.shape[0] // 2
-    for r, (x, out) in enumerate(((keep_in, keep), (send_in, send))):
-        out[:block, :] = x[:block, :] + dot(turned[aligned(own_half() ^ r, block), : 4 * n], held[...], NN)
-        out[block:, :] = x[block:, :]
+    part = block // CHUNKS
+    for r, x in enumerate((keep_in, send_in)):
+        added = dot(turned[aligned(own_half() ^ r, block), :], held[...], NN)
+        for c, out in enumerate(outs[r * CHUNKS : (r + 1) * CHUNKS]):
+            out[:part, :] = x[c * part : (c + 1) * part, :] + added[c * part : (c + 1) * part, :]
+            if c == 0:
+                out[part:, :] = x[block:, :]
 
 
 def rows_body(size, *refs):
@@ -301,18 +312,17 @@
 
 
 def place_body(size, *refs):
-    blocks, (enc_grad, rel_grad) = refs[:8], refs[8:]
-    block = enc_grad.shape[0] // 2
+    blocks, (enc_grad, rel_grad) = refs[:-2], refs[-2:]
+    part = enc_grad.shape[0] // 2 // CHUNKS
     me = own_quarter(size)
     n_rel = rel_grad.shape[0]
-    for r in range(2):
-        for j in range(4):
-            x = blocks[r * 4 + j]
-            lanes = aligned(me ^ APART[j], x.shape[1])
-            enc_grad[aligned(own_half() ^ r, block), lanes] = x[:block, :]
-            if r == 0:
-                for k in range(n_rel):
-                    rel_grad[k : k + 1, lanes] = x[pl.ds(block + lax.axis_index("rel") * n_rel + k, 1), :]
+    for at, x in enumerate(blocks):
+        r, c, j = at // (4 * CHUNKS), at // 4 % CHUNKS, at % 4
+        lanes = aligned(me ^ APART[j], x.shape[1])
+        enc_grad[aligned((own_half() ^ r) * CHUNKS + c, part), lanes] = x[:part, :]
+        if r == 0 and c == 0:
+            for k in range(n_rel):
+                rel_grad[k : k + 1, lanes] = x[pl.ds(part + lax.axis_index("rel") * n_rel + k, 1), :]
 
 
 def shards(src_feat, tgt_feat, enc_weight, rel_shift, edge_src, edge_tgt, rel_hot, neg_idx, edge_label):
@@ -327,7 +337,6 @@
     fields, _ = field_starts(edges, negs)
     rows = task_rows(edges, negs, emb)
     cfg = (fields, rows, s_rows, t_rows, n_rel, emb**-0.5, groups, negs, buckets)
-    n = s_rows + t_rows
     wide = emb // 4
 
     def met(x, mask):
@@ -348,34 +357,40 @@
         return [parts[0], met(parts[1], 1), met(parts[2], half), met(parts[3], half + 1)]
 
     which = sum(k * rel_hot[0, 0, :, k, :] for k in range(1, n_rel))
-    own, s_act, feats = call(
+    own, s_act = call(
         functools.partial(first_body, fields, rows),
-        [shaped((s_rows + slots * rows + 16, emb), BF16), shaped((s_rows, emb)), shaped((n, feat), BF16)],
-        [src_feat, tgt_feat, enc_weight, edge_src, edge_tgt, which, neg_idx, edge_label, rel_shift],
+        [shaped((s_rows + slots * rows + 16, emb), BF16), shaped((s_rows, emb))],
+        [src_feat, enc_weight, edge_src, edge_tgt, which, neg_idx, edge_label, rel_shift],
         scratch=[pltpu.VMEM((slots * rows, emb), F32)],
         flops=2 * s_rows * feat * emb,
     )
     first = around(own)
-    f_high = met(feats, half)
-    f_low = met(feats, 1)
-    f_far = met(f_high, 1)
-    tgt, act, turned = call(
-        functools.partial(prepare_body, buckets, s_rows),
-        [shaped((4 * t_rows, emb), BF16), shaped((4 * t_rows, wide)), shaped((feat, 4 * n), BF16)],
-        [feats, f_low, f_high, f_far, enc_weight],
-        scratch=[pltpu.VMEM((4 * n, feat), BF16)],
-        flops=8 * n * feat * emb,
+
+    def fetched(x):
+        high = met(x, half)
+        return [x, met(x, 1), high, met(high, 1)]
+
+    t_feats, s_feats = fetched(tgt_feat), fetched(src_feat)
+    (tgt,) = call(
+        encode_body,
+        [shaped((4 * t_rows, emb), BF16)],
+        [*t_feats, enc_weight],
+        scratch=[pltpu.VMEM((4 * t_rows, feat), BF16)],
+        flops=8 * t_rows * feat * emb,
     )
     queries = n_rel * groups * s_rows
-    *t_parts, s_keep, s_send = call(
+    tgt, s_feats = lax.optimization_barrier((tgt, s_feats))
+    parts = call(
         functools.partial(meets_body, cfg),
-        [shaped((4 * t_rows + 16, wide))] * 4 + [shaped((groups // 2 * s_rows, emb))] * 2,
+        [shaped((4 * t_rows + 16, wide))] * 4 + [shaped((s_rows, emb))] * groups,
         [*first, tgt],
         in_specs=[ANY] * 5 + [VMEM],
         scratch=[
             pltpu.VMEM((groups * s_rows, emb), BF16),
             pltpu.VMEM((groups, slots * rows + 16, emb), BF16),
             pltpu.VMEM((queries, emb), BF16),
+            pltpu.VMEM((queries, emb), BF16),
+            pltpu.VMEM((8 * t_rows, queries), BF16),
             pltpu.VMEM((8 * t_rows, queries), BF16),
             pltpu.VMEM((8 * t_rows, emb), F32),
             pltpu.VMEM((4 * t_rows, groups * s_rows), F32),
@@ -385,45 +400,59 @@
         ],
         flops=12e9,
     )
-    s_recv = crossed(s_send, 1)
+    t_parts, s_parts = parts[:4], parts[4:]
+    s_parts = [s_parts[0], *(crossed(s_parts[mask], mask) for mask in range(1, groups))]
     t_recv, t_next = met(t_parts[1], 1), met(t_parts[3], 1)
     t_last = met(t_parts[2] + t_next, half)
-    s_last = crossed(s_keep[s_rows:] + s_recv[s_rows:], 2)
+    s_feats, t_recv = lax.optimization_barrier((s_feats, t_recv))
+    act, s_turned, t_turned = call(
+        functools.partial(prepare_body, buckets),
+        [shaped((4 * t_rows, wide)), shaped((feat, 4 * s_rows), BF16), shaped((feat, 4 * t_rows), BF16)],
+        [*s_feats, *t_feats, enc_weight],
+        scratch=[pltpu.VMEM((4 * s_rows, feat), BF16), pltpu.VMEM((4 * t_rows, feat), BF16)],
+        flops=8 * t_rows * feat * wide,
+    )
+    s_parts, act = lax.optimization_barrier((s_parts, act))
     part = feat // 2
+    src_grad, *d_parts = call(
+        functools.partial(source_body, buckets),
+        [shaped((s_rows, emb))] + [shaped((s_rows, wide), BF16)] * 4,
+        [*s_parts, s_act],
+    )
+    d_parts, t_last = lax.optimization_barrier((d_parts, t_last))
     keep, send, *g_parts = call(
         functools.partial(target_body, buckets),
         [shaped((part + 16, wide))] * 2 + [shaped((t_rows, wide))] * 4,
-        [t_parts[0], t_recv, t_last, act, turned],
+        [t_parts[0], t_recv, t_last, act, t_turned],
         flops=8 * t_rows * feat * wide,
     )
-    keep, send, s_last = lax.optimization_barrier((keep, send, s_last))
-    src_grad, *d_parts = call(
-        functools.partial(source_body, buckets),
-        [shaped((s_rows, emb))] + [shaped((s_rows, wide), BF16)] * 4,
-        [s_keep, s_recv, s_last, s_act],
-    )
-    keep, send = call(
+    d_parts = shared(d_parts)
+    piece = part // CHUNKS
+    sizes = [shaped((piece + (16 if c == 0 else 0), wide)) for c in range(CHUNKS)] * 2
+    halves = call(
         functools.partial(join_body, buckets),
-        [shaped((part + 16, wide))] * 2,
-        [keep, send, turned, *shared(d_parts)],
+        sizes,
+        [keep, send, s_turned, *d_parts],
         scratch=[pltpu.VMEM((4 * s_rows, wide), BF16)],
         flops=8 * s_rows * feat * wide,
     )
-    got = met(send, 2)
-    g_parts, got = lax.optimization_barrier((shared(g_parts), got))
-    joint = keep + got
+    got = [met(x, 2) for x in halves[CHUNKS:]]
+    g_parts, got[0] = lax.optimization_barrier((shared(g_parts), got[0]))
     (tgt_grad,) = call(functools.partial(rows_body, buckets), [shaped((t_rows, emb))], g_parts)
-    for bit in range(2, buckets.bit_length() - 2):
-        joint = joint + met(joint, 1 << bit)
-    got = crossed(joint, 1)
-    tgt_grad, got = lax.optimization_barrier((tgt_grad, got))
-    joint = joint + got
-    joint = joint + crossed(joint, 3)
-    same = [joint, met(joint, half), met(joint, 2), met(joint, half + 2)]
-    other = [met(x, 1) for x in same]
-    blocks = [same[0], other[0], same[1], other[1], same[2], other[2], same[3], other[3]]
+    blocks = [[], []]
+    for c in range(CHUNKS):
+        joint = halves[c] + got[c]
+        for bit in range(2, buckets.bit_length() - 2):
+            joint = joint + met(joint, 1 << bit)
+        joint = joint + crossed(joint, 1)
+        if c == 0:
+            tgt_grad, joint = lax.optimization_barrier((tgt_grad, joint))
+        joint = joint + crossed(joint, 3)
+        for r, same in ((0, [joint, met(joint, half)]), (1, [met(joint, 2), met(joint, half + 2)])):
+            other = [met(x, 1) for x in same]
+            blocks[r] += [same[0], other[0], same[1], other[1]]
     enc_grad, rel_grad = call(
-        functools.partial(place_body, buckets), [shaped((feat, emb)), shaped((n_rel, emb))], blocks
+        functools.partial(place_body, buckets), [shaped((feat, emb)), shaped((n_rel, emb))], [*blocks[0], *blocks[1]]
     )
     return (src_grad, tgt_grad, rel_grad, enc_grad)
 

time: 118 us -> 117 us (level)
  waiting for transfers between devices: 50.3 us -> 32.7 us
  starting transfers between devices: 23.4 us -> 38.5 us
  Pallas kernels: 33.1 us -> 35.4 us
    ppermute x4 -> x7, waiting for transfers between devices: 20 us -> 9.25 us  [crossed(): return lax.ppermute(x, 'rel', [(i, i ^ mask) for i in range(groups)])]
    ppermute x4 -> x7, starting transfers between devices: 3.13 us -> 9.96 us  [crossed(): return lax.ppermute(x, 'rel', [(i, i ^ mask) for i in range(groups)])]
    ppermute x20 -> x31, starting transfers between devices: 13.9 us -> 20.6 us  [met(): return lax.ppermute(x, 'bucket', [(i, i ^ mask) for i in range(buckets)])]
    ppermute x20 -> x31, waiting for transfers between devices: 24.5 us -> 20.1 us  [met(): return lax.ppermute(x, 'bucket', [(i, i ^ mask) for i in range(buckets)])]
    ppermute x4, waiting for transfers between devices: 5.8 us -> 3.36 us  [ring(): lax.ppermute(x, 'rel', [(i, (i - step) % groups) for i in range(groups)])]
    pallas_call x8 -> x9, Pallas kernels: 33.1 us -> 35.4 us  [call(): pl.pallas_call(body, out_shape=tuple(outs), in_specs=in_specs or [VMEM] *...]
    ppermute x4, starting transfers between devices: 6.39 us -> 7.92 us  [ring(): lax.ppermute(x, 'rel', [(i, (i - step) % groups) for i in range(groups)])]
    unnamed x56 -> x74, local copies, waits for them, and re-layouts: 4.77 us -> 4.57 us
  transfers between devices with their start and end apart: 28 -> 42, of which waited for: 19 -> 17; matrix products, arithmetic and copies ran while one was open for 2% -> 4% of each run, Pallas kernels for 7% -> 13%
where the time goes in v1:
time: 117 us; the launch traced here: 116 us
  starting transfers between devices  38.5 us (33%)
  Pallas kernels  35.4 us (30%)
  waiting for transfers between devices  32.7 us (28%)
  local copies, waits for them, and re-layouts  4.58 us (4%)
  other arithmetic  4.27 us (4%)
    pallas_call x9, Pallas kernels, call(): pl.pallas_call(body, out_shape=tuple(outs), in_specs=in_specs or [VMEM] *...  35.4 us
    ppermute x31, starting transfers between devices, met(): return lax.ppermute(x, 'bucket', [(i, i ^ mask) for i in range(buckets)])  20.6 us
    ppermute x31, waiting for transfers between devices, met(): return lax.ppermute(x, 'bucket', [(i, i ^ mask) for i in range(buckets)])  20.1 us
    ppermute x7, starting transfers between devices, crossed(): return lax.ppermute(x, 'rel', [(i, i ^ mask) for i in range(groups)])  9.96 us
    ppermute x7, waiting for transfers between devices, crossed(): return lax.ppermute(x, 'rel', [(i, i ^ mask) for i in range(groups)])  9.25 us
    ppermute x4, starting transfers between devices, ring(): lax.ppermute(x, 'rel', [(i, (i - step) % groups) for i in range(groups)])  7.92 us
    unnamed x74, local copies, waits for them, and re-layouts  4.57 us
    ppermute x4, waiting for transfers between devices, ring(): lax.ppermute(x, 'rel', [(i, (i - step) % groups) for i in range(groups)])  3.36 us
  transfers between devices with their start and end apart: 42, of which 17 were waited for; matrix products, arithmetic and copies ran while one was open for 4% of the time, Pallas kernels for 13%

profile of v1, /device:TPU:0, one launch (start us, length us, event | category | flops | bytes accessed | tf_op | source)
XLA Modules:
  0.0 116.4 jit_solution(17379065416586538342)
XLA Ops:
  0.6 3.1 %collective-permute-start.5 = (bf16[128,768]{1,0:T(8,128)(2,1)}, bf16[128,768]{1,0:T(8,128)(2,1)S(1)}, u32[]{:S(2)}, u32[]{:S(2)}) collective-permute-start(bf16[128,768]{1,0:T(8,128)(2,1)} %refs_4_.1), channel_id=1, source_target_pairs={{0,16},{4,20},{8,24},{12,28},{16,0},{20,4},{24,8},{28,12},{1,17},{... | collective-permute-start | bytes 589832 | tf_op jit(solution)/shard_map/ppermute | solution.py:343
  3.7 5.1 %collective-permute-done.5.high.refs_6_ = bf16[128,768]{1,0:T(8,128)(2,1)S(1)} collective-permute-done((bf16[128,768]{1,0:T(8,128)(2,1)}, bf16[128,768]{1,0:T(8,128)(2,1)S(1)}, u32[]{:S(2)}, u32[]{:S(2)}) %collective-permute-start.5) | collective-permute-done | bytes 196640 | tf_op jit(solution)/shard_map/ppermute | solution.py:343
  8.8 1.4 %add_bitcast_fusion.rel = s32[4,768]{1,0:T(4,128)} fusion(s32[1,1,4,3,768]{4,2,3,1,0:T(4,128)} %param.15), kind=kLoop, calls=%fused_computation | loop fusion | flops 6144 | bytes 36864 | tf_op jit(solution)/shard_map/add | solution.py:359
  10.2 2.1 %shard_map.120 = (bf16[112,512]{1,0:T(8,128)(2,1)}, f32[64,512]{1,0:T(8,128)}) custom-call(bf16[64,768]{1,0:T(8,128)(2,1)} %refs_0_, bf16[768,512]{1,0:T(8,128)(2,1)} %refs_8_.1, s32[1,1,4,768]{3,2,1,0:T(4,128)} %src.1, s32[1,1,4,768]{3,2,1,0:T(4,128)} %tgt.1, s32[4,768]{1,0:T(4,128)} %add_bitcast_fusion.rel, s32[1,1,4,128]{3,2,1,0:T(4,128)} %neg.1, ...), custom_call_target="tpu_custom_call" | custom-call | flops 50331648 | bytes 1184768 | tf_op jit(solution)/shard_map/pallas_call | solution.py:31
  12.3 1.8 %collective-permute-start.1 = (bf16[112,512]{1,0:T(8,128)(2,1)}, bf16[112,512]{1,0:T(8,128)(2,1)S(1)}, u32[]{:S(2)}, u32[]{:S(2)}) collective-permute-start(bf16[112,512]{1,0:T(8,128)(2,1)} %get-tuple-element.61.own), channel_id=1, source_target_pairs={{0,1},{1,2},{2,3},{3,0},{4,5},{5,6},{6,7},{7,4},{8,9},{9,10},{10,1... | collective-permute-start | bytes 344072 | tf_op jit(solution)/shard_map/ppermute | solution.py:346
  14.1 1.5 %collective-permute-start.8 = (bf16[64,768]{1,0:T(8,128)(2,1)}, bf16[64,768]{1,0:T(8,128)(2,1)S(1)}, u32[]{:S(2)}, u32[]{:S(2)}) collective-permute-start(bf16[64,768]{1,0:T(8,128)(2,1)} %refs_0_), channel_id=1, source_target_pairs={{0,16},{4,20},{8,24},{12,28},{16,0},{20,4},{24,8},{28,12},{1,17},{... | collective-permute-start | bytes 294920 | tf_op jit(solution)/shard_map/ppermute | solution.py:343
  15.6 2.2 %collective-permute-start = (bf16[112,512]{1,0:T(8,128)(2,1)}, bf16[112,512]{1,0:T(8,128)(2,1)S(1)}, u32[]{:S(2)}, u32[]{:S(2)}) collective-permute-start(bf16[112,512]{1,0:T(8,128)(2,1)} %get-tuple-element.61.own), channel_id=1, source_target_pairs={{0,3},{1,0},{2,1},{3,2},{4,7},{5,4},{6,5},{7,6},{8,11},{9,8},{10,9... | collective-permute-start | bytes 344072 | tf_op jit(solution)/shard_map/ppermute | solution.py:346
  17.9 1.3 %collective-permute-done.8.refs_2_ = bf16[64,768]{1,0:T(8,128)(2,1)S(1)} collective-permute-done((bf16[64,768]{1,0:T(8,128)(2,1)}, bf16[64,768]{1,0:T(8,128)(2,1)S(1)}, u32[]{:S(2)}, u32[]{:S(2)}) %collective-permute-start.8) | collective-permute-done | bytes 98336 | tf_op jit(solution)/shard_map/ppermute | solution.py:343
  19.2 1.0 collective-permute-done.1.minus
  20.2 2.3 %collective-permute-done.plus = bf16[112,512]{1,0:T(8,128)(2,1)S(1)} collective-permute-done((bf16[112,512]{1,0:T(8,128)(2,1)}, bf16[112,512]{1,0:T(8,128)(2,1)S(1)}, u32[]{:S(2)}, u32[]{:S(2)}) %collective-permute-start) | collective-permute-done | bytes 114720 | tf_op jit(solution)/shard_map/ppermute | solution.py:346
  22.6 0.6 collective-permute-start.3
  23.2 3.3 %collective-permute-start.2 = (bf16[56,512]{1,0:T(8,128)(2,1)S(1)}, bf16[56,512]{1,0:T(8,128)(2,1)S(1)}, u32[]{:S(2)}, u32[]{:S(2)}) collective-permute-start(bf16[56,512]{1,0:T(8,128)(2,1)S(1)} %slice.16), channel_id=1, source_target_pairs={{0,3},{1,0},{2,1},{3,2},{4,7},{5,4},{6,5},{7,6},{8,11},{9,8},{10,9... | collective-permute-start | bytes 172040 | tf_op jit(solution)/shard_map/ppermute | solution.py:346
  26.5 0.7 copy-done.2
  27.2 2.9 %shard_map.121.tgt = bf16[512,512]{1,0:T(8,128)(2,1)} custom-call(bf16[128,768]{1,0:T(8,128)(2,1)} %refs_4_.1, bf16[128,768]{1,0:T(8,128)(2,1)} %copy-done.1, bf16[128,768]{1,0:T(8,128)(2,1)} %copy-done, bf16[128,768]{1,0:T(8,128)(2,1)} %copy-done.2, bf16[768,512]{1,0:T(8,128)(2,1)} %refs_8_.1), custom_call_target="tpu_custom_call" | custom-call | flops 402653184 | bytes 2097152 | tf_op jit(solution)/shard_map/pallas_call | solution.py:31
  30.1 0.6 copy-done.35
  30.8 0.6 copy-done.36
  31.4 15.7 %shard_map.122 = (f32[528,128]{1,0:T(8,128)}, f32[528,128]{1,0:T(8,128)}, f32[528,128]{1,0:T(8,128)}, f32[528,128]{1,0:T(8,128)}, f32[64,512]{1,0:T(8,128)}, /*i...) custom-call(bf16[112,512]{1,0:T(8,128)(2,1)} %get-tuple-element.61.own, bf16[112,512]{1,0:T(8,128)(2,1)} %copy-done.31, ...), custom_call_target="tpu_custom_call" | custom-call | flops 12000000000 | bytes 2588672 | tf_op jit(solution)/shard_map/pallas_call | solution.py:31
  47.2 0.5 collective-permute-start.13
  47.7 1.2 %collective-permute-done.14 = f32[528,128]{1,0:T(8,128)S(1)} collective-permute-done((f32[528,128]{1,0:T(8,128)}, f32[528,128]{1,0:T(8,128)S(1)}, u32[]{:S(2)}, u32[]{:S(2)}) %collective-permute-start.14) | collective-permute-done | bytes 270368 | tf_op jit(solution)/shard_map/ppermute | solution.py:343
  48.9 1.0 add.28
  49.9 1.2 %collective-permute-start.15 = (f32[528,128]{1,0:T(8,128)S(1)}, f32[528,128]{1,0:T(8,128)S(1)}, u32[]{:S(2)}, u32[]{:S(2)}) collective-permute-start(f32[528,128]{1,0:T(8,128)S(1)} %add.28), channel_id=1, source_target_pairs={{0,16},{4,20},{8,24},{12,28},{16,0},{20,4},{24,8},{28,12},{1,17},{... | collective-permute-start | bytes 811016 | tf_op jit(solution)/shard_map/ppermute | solution.py:343
  51.2 2.3 %collective-permute-start.11 = (f32[64,512]{1,0:T(8,128)}, f32[64,512]{1,0:T(8,128)S(1)}, u32[]{:S(2)}, u32[]{:S(2)}) collective-permute-start(f32[64,512]{1,0:T(8,128)} %get-tuple-element.65), channel_id=1, source_target_pairs={{0,2},{1,3},{2,0},{3,1},{4,6},{5,7},{6,4},{7,5},{8,10},{9,11},{10,... | collective-permute-start | bytes 393224 | tf_op jit(solution)/shard_map/ppermute | solution.py:349
  53.4 2.1 %collective-permute-start.12 = (f32[64,512]{1,0:T(8,128)}, f32[64,512]{1,0:T(8,128)S(1)}, u32[]{:S(2)}, u32[]{:S(2)}) collective-permute-start(f32[64,512]{1,0:T(8,128)} %get-tuple-element.66), channel_id=1, source_target_pairs={{0,3},{1,2},{2,1},{3,0},{4,7},{5,6},{6,5},{7,4},{8,11},{9,10},{10,... | collective-permute-start | bytes 393224 | tf_op jit(solution)/shard_map/ppermute | solution.py:349
  55.6 3.1 %shard_map.123 = (f32[512,128]{1,0:T(8,128)}, bf16[768,256]{1,0:T(8,128)(2,1)}, bf16[768,512]{1,0:T(8,128)(2,1)}) custom-call(bf16[64,768]{1,0:T(8,128)(2,1)} %refs_0_, bf16[64,768]{1,0:T(8,128)(2,1)} %copy-done.25, bf16[64,768]{1,0:T(8,128)(2,1)} %copy-done.24, bf16[64,768]{1,0:T(8,128)(2,1)} %copy-done.26, bf16[128,768]{1,0:T(8,128)(2,1)} %refs_4_.1, ...), custom_call_target="tpu_custom_call" | custom-call | flops 100663296 | bytes 3407872 | tf_op jit(solution)/shard_map/pallas_call | solution.py:31
  58.7 5.6 %collective-permute-done.11.c = f32[64,512]{1,0:T(8,128)S(1)} collective-permute-done((f32[64,512]{1,0:T(8,128)}, f32[64,512]{1,0:T(8,128)S(1)}, u32[]{:S(2)}, u32[]{:S(2)}) %collective-permute-start.11) | collective-permute-done | bytes 131104 | tf_op jit(solution)/shard_map/ppermute | solution.py:349
  64.3 0.6 copy-done.8
  65.0 1.9 %shard_map.124 = (f32[64,512]{1,0:T(8,128)}, bf16[64,128]{1,0:T(8,128)(2,1)}, bf16[64,128]{1,0:T(8,128)(2,1)}, bf16[64,128]{1,0:T(8,128)(2,1)}, bf16[64,128]{1,0:T(8,128)(2,1)}) custom-call(f32[64,512]{1,0:T(8,128)} %get-tuple-element.77.a, f32[64,512]{1,0:T(8,128)} %copy-done.7, f32[64,512]{1,0:T(8,128)} %copy-done.8, f32[64,512]{1,0:T(8,128)} %copy-done.9, ...), custom_call_target="tpu_custom_call" | custom-call | bytes 851968 | tf_op jit(solution)/shard_map/pallas_call | solution.py:31
  67.0 0.9 collective-permute-start.20
  67.9 0.9 collective-permute-start.21
  68.8 2.9 %shard_map.125 = (f32[400,128]{1,0:T(8,128)}, f32[400,128]{1,0:T(8,128)}, f32[128,128]{1,0:T(8,128)}, f32[128,128]{1,0:T(8,128)}, f32[128,128]{1,0:T(8,128)}, /*index=5*/f32[128,128]{1,0:T(8,128)}) custom-call(f32[528,128]{1,0:T(8,128)} %get-tuple-element.83.keep, f32[528,128]{1,0:T(8,128)} %copy-done.5, f32[528,128]{1,0:T(8,128)} %copy-done.6, ...), custom_call_target="tpu_custom_call" | custom-call | flops 100663296 | bytes 2531328 | tf_op jit(solution)/shard_map/pallas_call | solution.py:31
  71.8 0.6 copy-done.32
  72.4 2.2 %shard_map.126 = (f32[208,128]{1,0:T(8,128)}, f32[192,128]{1,0:T(8,128)}, f32[208,128]{1,0:T(8,128)}, f32[192,128]{1,0:T(8,128)}) custom-call(f32[400,128]{1,0:T(8,128)} %get-tuple-element.98.keep_in, f32[400,128]{1,0:T(8,128)} %get-tuple-element.99.send_in, bf16[768,256]{1,0:T(8,128)(2,1)} %get-tuple-element.100.turned, ...), custom_call_target="tpu_custom_call" | custom-call | flops 50331648 | bytes 1277952 | tf_op jit(solution)/shard_map/pallas_call | solution.py:31
  74.6 1.5 %collective-permute-start.28 = (f32[192,128]{1,0:T(8,128)}, f32[192,128]{1,0:T(8,128)S(1)}, u32[]{:S(2)}, u32[]{:S(2)}) collective-permute-start(f32[192,128]{1,0:T(8,128)} %get-tuple-element.115), channel_id=1, source_target_pairs={{0,8},{4,12},{8,0},{12,4},{16,24},{20,28},{24,16},{28,20},{1,9},{5... | collective-permute-start | bytes 294920 | tf_op jit(solution)/shard_map/ppermute | solution.py:343
  76.1 0.5 collective-permute-start.22
  76.7 3.9 %collective-permute-done.28 = f32[192,128]{1,0:T(8,128)S(1)} collective-permute-done((f32[192,128]{1,0:T(8,128)}, f32[192,128]{1,0:T(8,128)S(1)}, u32[]{:S(2)}, u32[]{:S(2)}) %collective-permute-start.28) | collective-permute-done | bytes 98336 | tf_op jit(solution)/shard_map/ppermute | solution.py:343
  80.5 0.9 add.32
  81.4 2.3 %collective-permute-start.29 = (f32[192,128]{1,0:T(8,128)S(1)}, f32[192,128]{1,0:T(8,128)S(1)}, u32[]{:S(2)}, u32[]{:S(2)}) collective-permute-start(f32[192,128]{1,0:T(8,128)S(1)} %add.32), channel_id=1, source_target_pairs={{0,1},{1,0},{2,3},{3,2},{4,5},{5,4},{6,7},{7,6},{8,9},{9,8},{10,11... | collective-permute-start | bytes 294920 | tf_op jit(solution)/shard_map/ppermute | solution.py:349
  83.7 0.8 collective-permute-start.17
  84.6 1.0 collective-permute-start.18
  85.6 3.3 %collective-permute-done.17.refs_2_ = f32[128,128]{1,0:T(8,128)S(1)} collective-permute-done((f32[128,128]{1,0:T(8,128)}, f32[128,128]{1,0:T(8,128)S(1)}, u32[]{:S(2)}, u32[]{:S(2)}) %collective-permute-start.17) | collective-permute-done | bytes 65568 | tf_op jit(solution)/shard_map/ppermute | solution.py:343
  88.9 0.5 collective-permute-done.18.refs_3_
  89.4 0.9 add.29
  90.4 1.8 %collective-permute-start.30 = (f32[192,128]{1,0:T(8,128)S(1)}, f32[192,128]{1,0:T(8,128)S(1)}, u32[]{:S(2)}, u32[]{:S(2)}) collective-permute-start(f32[192,128]{1,0:T(8,128)S(1)} %add.33), channel_id=1, source_target_pairs={{0,3},{1,2},{2,1},{3,0},{4,7},{5,6},{6,5},{7,4},{8,11},{9,10},{10,... | collective-permute-start | bytes 294920 | tf_op jit(solution)/shard_map/ppermute | solution.py:349
  92.2 1.7 %shard_map.127 = f32[128,512]{1,0:T(8,128)} custom-call(f32[128,128]{1,0:T(8,128)} %get-tuple-element.106.refs_0_, f32[128,128]{1,0:T(8,128)} %copy-done.27, f32[128,128]{1,0:T(8,128)} %copy-done.28, f32[128,128]{1,0:T(8,128)} %copy-done.29), custom_call_target="tpu_custom_call" | custom-call | bytes 524288 | tf_op jit(solution)/shard_map/pallas_call | solution.py:31
  93.9 2.0 %collective-permute-done.23 = f32[208,128]{1,0:T(8,128)S(1)} collective-permute-done((f32[208,128]{1,0:T(8,128)S(1)}, f32[208,128]{1,0:T(8,128)S(1)}, u32[]{:S(2)}, u32[]{:S(2)}) %collective-permute-start.23) | collective-permute-done | bytes 106528 | tf_op jit(solution)/shard_map/ppermute | solution.py:349
  95.9 1.4 %collective-permute-start.24 = (f32[208,128]{1,0:T(8,128)S(1)}, f32[208,128]{1,0:T(8,128)S(1)}, u32[]{:S(2)}, u32[]{:S(2)}) collective-permute-start(f32[208,128]{1,0:T(8,128)S(1)} %add.30), channel_id=1, source_target_pairs={{0,3},{1,2},{2,1},{3,0},{4,7},{5,6},{6,5},{7,4},{8,11},{9,10},{10,... | collective-permute-start | bytes 319496 | tf_op jit(solution)/shard_map/ppermute | solution.py:349
  97.4 0.4 collective-permute-done.30
  97.8 1.8 %collective-permute-start.40 = (f32[192,128]{1,0:T(8,128)S(1)}, f32[192,128]{1,0:T(8,128)S(1)}, u32[]{:S(2)}, u32[]{:S(2)}) collective-permute-start(f32[192,128]{1,0:T(8,128)S(1)} %add.34.refs_4_), channel_id=1, source_target_pairs={{0,24},{4,28},{8,16},{12,20},{16,8},{20,12},{24,0},{28,4},{1,25},{... | collective-permute-start | bytes 294920 | tf_op jit(solution)/shard_map/ppermute | solution.py:343
  99.6 0.5 collective-permute-start.38
  100.1 1.2 %collective-permute-start.32 = (f32[192,128]{1,0:T(8,128)S(1)}, f32[192,128]{1,0:T(8,128)S(1)}, u32[]{:S(2)}, u32[]{:S(2)}) collective-permute-start(f32[192,128]{1,0:T(8,128)S(1)} %add.34.refs_4_), channel_id=1, source_target_pairs={{0,16},{4,20},{8,24},{12,28},{16,0},{20,4},{24,8},{28,12},{1,17},{... | collective-permute-start | bytes 294920 | tf_op jit(solution)/shard_map/ppermute | solution.py:343
  101.3 1.3 %collective-permute-done.24 = f32[208,128]{1,0:T(8,128)S(1)} collective-permute-done((f32[208,128]{1,0:T(8,128)S(1)}, f32[208,128]{1,0:T(8,128)S(1)}, u32[]{:S(2)}, u32[]{:S(2)}) %collective-permute-start.24) | collective-permute-done | bytes 106528 | tf_op jit(solution)/shard_map/ppermute | solution.py:349
  102.6 1.8 %collective-permute-start.36 = (f32[208,128]{1,0:T(8,128)S(1)}, f32[208,128]{1,0:T(8,128)S(1)}, u32[]{:S(2)}, u32[]{:S(2)}) collective-permute-start(f32[208,128]{1,0:T(8,128)S(1)} %add.31.refs_0_), channel_id=1, source_target_pairs={{0,24},{4,28},{8,16},{12,20},{16,8},{20,12},{24,0},{28,4},{1,25},{... | collective-permute-start | bytes 319496 | tf_op jit(solution)/shard_map/ppermute | solution.py:343
  104.5 1.2 %collective-permute-start.34 = (f32[208,128]{1,0:T(8,128)S(1)}, f32[208,128]{1,0:T(8,128)S(1)}, u32[]{:S(2)}, u32[]{:S(2)}) collective-permute-start(f32[208,128]{1,0:T(8,128)S(1)} %add.31.refs_0_), channel_id=1, source_target_pairs={{0,8},{4,12},{8,0},{12,4},{16,24},{20,28},{24,16},{28,20},{1,9},{5... | collective-permute-start | bytes 319496 | tf_op jit(solution)/shard_map/ppermute | solution.py:343
  105.7 0.7 collective-permute-start.26
  106.4 0.5 collective-permute-start.41
  106.9 2.0 %collective-permute-done.36.refs_10_ = f32[208,128]{1,0:T(8,128)S(1)} collective-permute-done((f32[208,128]{1,0:T(8,128)S(1)}, f32[208,128]{1,0:T(8,128)S(1)}, u32[]{:S(2)}, u32[]{:S(2)}) %collective-permute-start.36) | collective-permute-done | bytes 106528 | tf_op jit(solution)/shard_map/ppermute | solution.py:343
  108.9 0.5 collective-permute-done.34.refs_8_
  109.4 1.0 collective-permute-done.26.refs_2_
  110.4 0.5 collective-permute-start.39
  111.0 0.9 collective-permute-done.39.refs_13_
  111.9 0.4 collective-permute-done.33.refs_7_
  112.5 0.3 copy-done.23
  113.0 0.6 copy-done.16
  113.6 2.8 %shard_map.128 = (f32[768,512]{1,0:T(8,128)}, f32[3,512]{1,0:T(4,128)}) custom-call(f32[208,128]{1,0:T(8,128)} %copy-done.3, f32[208,128]{1,0:T(8,128)} %copy-done.13, f32[208,128]{1,0:T(8,128)} %copy-done.12, f32[208,128]{1,0:T(8,128)} %copy-done.16, f32[192,128]{1,0:T(8,128)} %copy-done.4, f32[192,128]{1,0:T(8,128)} %copy-done.20, f32[192,128]{1,0:T(8,128)} %copy-done.19, ...), custom_call_target="tpu_custom_call" | custom-call | bytes 3217408 | tf_op jit(solution)/shard_map/pallas_call | solution.py:31
  (113 shorter events, 0.9 us)
Async XLA Ops:
  0.6 8.2 %collective-permute-start.5 = (bf16[128,768]{1,0:T(8,128)(2,1)}, bf16[128,768]{1,0:T(8,128)(2,1)S(1)}, u32[]{:S(2)}, u32[]{:S(2)}) collective-permute-start(bf16[128,768]{1,0:T(8,128)(2,1)} %refs_4_.1), channel_id=1, source_target_pairs={{0,16},{4,20},{8,24},{12,28},{16,0},{20,4},{24,8},{28,12},{1,17},{... | collective-permute-start | bytes 589832 | tf_op jit(solution)/shard_map/ppermute | solution.py:343
  3.7 19.5 %collective-permute-start.4 = (bf16[128,768]{1,0:T(8,128)(2,1)}, bf16[128,768]{1,0:T(8,128)(2,1)S(1)}, u32[]{:S(2)}, u32[]{:S(2)}) collective-permute-start(bf16[128,768]{1,0:T(8,128)(2,1)} %refs_4_.1), channel_id=1, source_target_pairs={{0,4},{4,0},{8,12},{12,8},{16,20},{20,16},{24,28},{28,24},{1,5},{5... | collective-permute-start | bytes 589832 | tf_op jit(solution)/shard_map/ppermute | solution.py:343
  8.8 17.7 %copy-start = (bf16[128,768]{1,0:T(8,128)(2,1)}, bf16[128,768]{1,0:T(8,128)(2,1)S(1)}, u32[]{:S(2)}) copy-start(bf16[128,768]{1,0:T(8,128)(2,1)S(1)} %collective-permute-done.5.high.refs_6_) | copy-start | bytes 589828
  8.8 17.7 %collective-permute-start.6 = (bf16[128,768]{1,0:T(8,128)(2,1)S(1)}, bf16[128,768]{1,0:T(8,128)(2,1)S(1)}, u32[]{:S(2)}, u32[]{:S(2)}) collective-permute-start(bf16[128,768]{1,0:T(8,128)(2,1)S(1)} %collective-permute-done.5.high.refs_6_), channel_id=1, source_target_pairs={{0,4},{4,0},{8,12},{12,8},{16,20},{20,16},{24,28},{28,24},{1,5},{5... | collective-permute-start | bytes 589832 | tf_op jit(solution)/shard_map/ppermute | solution.py:343
  12.3 7.9 %collective-permute-start.1 = (bf16[112,512]{1,0:T(8,128)(2,1)}, bf16[112,512]{1,0:T(8,128)(2,1)S(1)}, u32[]{:S(2)}, u32[]{:S(2)}) collective-permute-start(bf16[112,512]{1,0:T(8,128)(2,1)} %get-tuple-element.61.own), channel_id=1, source_target_pairs={{0,1},{1,2},{2,3},{3,0},{4,5},{5,6},{6,7},{7,4},{8,9},{9,10},{10,1... | collective-permute-start | bytes 344072 | tf_op jit(solution)/shard_map/ppermute | solution.py:346
  14.1 5.1 %collective-permute-start.8 = (bf16[64,768]{1,0:T(8,128)(2,1)}, bf16[64,768]{1,0:T(8,128)(2,1)S(1)}, u32[]{:S(2)}, u32[]{:S(2)}) collective-permute-start(bf16[64,768]{1,0:T(8,128)(2,1)} %refs_0_), channel_id=1, source_target_pairs={{0,16},{4,20},{8,24},{12,28},{16,0},{20,4},{24,8},{28,12},{1,17},{... | collective-permute-start | bytes 294920 | tf_op jit(solution)/shard_map/ppermute | solution.py:343
  15.6 6.9 %collective-permute-start = (bf16[112,512]{1,0:T(8,128)(2,1)}, bf16[112,512]{1,0:T(8,128)(2,1)S(1)}, u32[]{:S(2)}, u32[]{:S(2)}) collective-permute-start(bf16[112,512]{1,0:T(8,128)(2,1)} %get-tuple-element.61.own), channel_id=1, source_target_pairs={{0,3},{1,0},{2,1},{3,2},{4,7},{5,4},{6,5},{7,6},{8,11},{9,8},{10,9... | collective-permute-start | bytes 344072 | tf_op jit(solution)/shard_map/ppermute | solution.py:346
  19.2 27.9 %copy-start.24 = (bf16[64,768]{1,0:T(8,128)(2,1)}, bf16[64,768]{1,0:T(8,128)(2,1)S(1)}, u32[]{:S(2)}) copy-start(bf16[64,768]{1,0:T(8,128)(2,1)S(1)} %collective-permute-done.8.refs_2_) | copy-start | bytes 294916
  19.2 10.8 %collective-permute-start.7 = (bf16[64,768]{1,0:T(8,128)(2,1)}, bf16[64,768]{1,0:T(8,128)(2,1)S(1)}, u32[]{:S(2)}, u32[]{:S(2)}) collective-permute-start(bf16[64,768]{1,0:T(8,128)(2,1)} %refs_0_), channel_id=1, source_target_pairs={{0,4},{4,0},{8,12},{12,8},{16,20},{20,16},{24,28},{28,24},{1,5},{5... | collective-permute-start | bytes 294920 | tf_op jit(solution)/shard_map/ppermute | solution.py:343
  20.2 9.9 %copy-start.30 = (bf16[112,512]{1,0:T(8,128)(2,1)}, bf16[112,512]{1,0:T(8,128)(2,1)S(1)}, u32[]{:S(2)}) copy-start(bf16[112,512]{1,0:T(8,128)(2,1)S(1)} %collective-permute-done.1.minus) | copy-start | bytes 344068
  20.2 9.8 %collective-permute-start.9 = (bf16[64,768]{1,0:T(8,128)(2,1)S(1)}, bf16[64,768]{1,0:T(8,128)(2,1)S(1)}, u32[]{:S(2)}, u32[]{:S(2)}) collective-permute-start(bf16[64,768]{1,0:T(8,128)(2,1)S(1)} %collective-permute-done.8.refs_2_), channel_id=1, source_target_pairs={{0,4},{4,0},{8,12},{12,8},{16,20},{20,16},{24,28},{28,24},{1,5},{5... | collective-permute-start | bytes 294920 | tf_op jit(solution)/shard_map/ppermute | solution.py:343
  22.6 7.5 %copy-start.31 = (bf16[112,512]{1,0:T(8,128)(2,1)}, bf16[112,512]{1,0:T(8,128)(2,1)S(1)}, u32[]{:S(2)}) copy-start(bf16[112,512]{1,0:T(8,128)(2,1)S(1)} %collective-permute-done.plus) | copy-start | bytes 344068
  22.6 7.5 %collective-permute-start.3 = (bf16[56,512]{1,0:T(8,128)(2,1)S(1)}, bf16[56,512]{1,0:T(8,128)(2,1)S(1)}, u32[]{:S(2)}, u32[]{:S(2)}) collective-permute-start(bf16[56,512]{1,0:T(8,128)(2,1)S(1)} %slice.17), channel_id=1, source_target_pairs={{0,1},{1,2},{2,3},{3,0},{4,5},{5,6},{6,7},{7,4},{8,9},{9,10},{10,1... | collective-permute-start | bytes 172040 | tf_op jit(solution)/shard_map/ppermute | solution.py:346
  23.2 3.3 %copy-start.1 = (bf16[128,768]{1,0:T(8,128)(2,1)}, bf16[128,768]{1,0:T(8,128)(2,1)S(1)}, u32[]{:S(2)}) copy-start(bf16[128,768]{1,0:T(8,128)(2,1)S(1)} %collective-permute-done.4.low.refs_5_) | copy-start | bytes 589828
  23.2 6.9 %collective-permute-start.2 = (bf16[56,512]{1,0:T(8,128)(2,1)S(1)}, bf16[56,512]{1,0:T(8,128)(2,1)S(1)}, u32[]{:S(2)}, u32[]{:S(2)}) collective-permute-start(bf16[56,512]{1,0:T(8,128)(2,1)S(1)} %slice.16), channel_id=1, source_target_pairs={{0,3},{1,0},{2,1},{3,2},{4,7},{5,4},{6,5},{7,6},{8,11},{9,8},{10,9... | collective-permute-start | bytes 172040 | tf_op jit(solution)/shard_map/ppermute | solution.py:346
  30.1 17.0 %copy-start.25 = (bf16[64,768]{1,0:T(8,128)(2,1)}, bf16[64,768]{1,0:T(8,128)(2,1)S(1)}, u32[]{:S(2)}) copy-start(bf16[64,768]{1,0:T(8,128)(2,1)S(1)} %collective-permute-done.7.refs_1_) | copy-start | bytes 294916
  30.1 17.0 %copy-start.26 = (bf16[64,768]{1,0:T(8,128)(2,1)}, bf16[64,768]{1,0:T(8,128)(2,1)S(1)}, u32[]{:S(2)}) copy-start(bf16[64,768]{1,0:T(8,128)(2,1)S(1)} %collective-permute-done.9.refs_3_) | copy-start | bytes 294916
  47.1 1.8 %collective-permute-start.14 = (f32[528,128]{1,0:T(8,128)}, f32[528,128]{1,0:T(8,128)S(1)}, u32[]{:S(2)}, u32[]{:S(2)}) collective-permute-start(f32[528,128]{1,0:T(8,128)} %get-tuple-element.90), channel_id=1, source_target_pairs={{0,4},{4,0},{8,12},{12,8},{16,20},{20,16},{24,28},{28,24},{1,5},{5... | collective-permute-start | bytes 811016 | tf_op jit(solution)/shard_map/ppermute | solution.py:343
  47.2 8.4 %collective-permute-start.13 = (f32[528,128]{1,0:T(8,128)}, f32[528,128]{1,0:T(8,128)S(1)}, u32[]{:S(2)}, u32[]{:S(2)}) collective-permute-start(f32[528,128]{1,0:T(8,128)} %get-tuple-element.71), channel_id=1, source_target_pairs={{0,4},{4,0},{8,12},{12,8},{16,20},{20,16},{24,28},{28,24},{1,5},{5... | collective-permute-start | bytes 811016 | tf_op jit(solution)/shard_map/ppermute | solution.py:343
  49.9 17.0 %collective-permute-start.15 = (f32[528,128]{1,0:T(8,128)S(1)}, f32[528,128]{1,0:T(8,128)S(1)}, u32[]{:S(2)}, u32[]{:S(2)}) collective-permute-start(f32[528,128]{1,0:T(8,128)S(1)} %add.28), channel_id=1, source_target_pairs={{0,16},{4,20},{8,24},{12,28},{16,0},{20,4},{24,8},{28,12},{1,17},{... | collective-permute-start | bytes 811016 | tf_op jit(solution)/shard_map/ppermute | solution.py:343
  51.2 7.5 %collective-permute-start.10 = (f32[64,512]{1,0:T(8,128)}, f32[64,512]{1,0:T(8,128)S(1)}, u32[]{:S(2)}, u32[]{:S(2)}) collective-permute-start(f32[64,512]{1,0:T(8,128)} %get-tuple-element.64), channel_id=1, source_target_pairs={{0,1},{1,0},{2,3},{3,2},{4,5},{5,4},{6,7},{7,6},{8,9},{9,8},{10,11... | collective-permute-start | bytes 393224 | tf_op jit(solution)/shard_map/ppermute | solution.py:349
  51.2 13.1 %collective-permute-start.11 = (f32[64,512]{1,0:T(8,128)}, f32[64,512]{1,0:T(8,128)S(1)}, u32[]{:S(2)}, u32[]{:S(2)}) collective-permute-start(f32[64,512]{1,0:T(8,128)} %get-tuple-element.65), channel_id=1, source_target_pairs={{0,2},{1,3},{2,0},{3,1},{4,6},{5,7},{6,4},{7,5},{8,10},{9,11},{10,... | collective-permute-start | bytes 393224 | tf_op jit(solution)/shard_map/ppermute | solution.py:349
  53.4 10.8 %collective-permute-start.12 = (f32[64,512]{1,0:T(8,128)}, f32[64,512]{1,0:T(8,128)S(1)}, u32[]{:S(2)}, u32[]{:S(2)}) collective-permute-start(f32[64,512]{1,0:T(8,128)} %get-tuple-element.66), channel_id=1, source_target_pairs={{0,3},{1,2},{2,1},{3,0},{4,7},{5,6},{6,5},{7,4},{8,11},{9,10},{10,... | collective-permute-start | bytes 393224 | tf_op jit(solution)/shard_map/ppermute | solution.py:349
  55.6 13.3 %copy-start.5 = (f32[528,128]{1,0:T(8,128)}, f32[528,128]{1,0:T(8,128)S(1)}, u32[]{:S(2)}) copy-start(f32[528,128]{1,0:T(8,128)S(1)} %collective-permute-done.13.recv) | copy-start | bytes 811012
  58.7 5.6 %copy-start.7 = (f32[64,512]{1,0:T(8,128)}, f32[64,512]{1,0:T(8,128)S(1)}, u32[]{:S(2)}) copy-start(f32[64,512]{1,0:T(8,128)S(1)} %collective-permute-done.10.b) | copy-start | bytes 393220
  66.9 4.9 %collective-permute-start.19 = (bf16[64,128]{1,0:T(8,128)(2,1)}, bf16[64,128]{1,0:T(8,128)(2,1)S(1)}, u32[]{:S(2)}, u32[]{:S(2)}) collective-permute-start(bf16[64,128]{1,0:T(8,128)(2,1)} %get-tuple-element.102), channel_id=1, source_target_pairs={{0,4},{4,0},{8,12},{12,8},{16,20},{20,16},{24,28},{28,24},{1,5},{5... | collective-permute-start | bytes 49160 | tf_op jit(solution)/shard_map/ppermute | solution.py:343
  67.0 4.8 %collective-permute-start.20 = (bf16[64,128]{1,0:T(8,128)(2,1)}, bf16[64,128]{1,0:T(8,128)(2,1)S(1)}, u32[]{:S(2)}, u32[]{:S(2)}) collective-permute-start(bf16[64,128]{1,0:T(8,128)(2,1)} %get-tuple-element.103), channel_id=1, source_target_pairs={{0,16},{4,20},{8,24},{12,28},{16,0},{20,4},{24,8},{28,12},{1,17},{... | collective-permute-start | bytes 49160 | tf_op jit(solution)/shard_map/ppermute | solution.py:343
  67.9 3.9 %collective-permute-start.21 = (bf16[64,128]{1,0:T(8,128)(2,1)}, bf16[64,128]{1,0:T(8,128)(2,1)S(1)}, u32[]{:S(2)}, u32[]{:S(2)}) collective-permute-start(bf16[64,128]{1,0:T(8,128)(2,1)} %get-tuple-element.104), channel_id=1, source_target_pairs={{0,20},{4,16},{8,28},{12,24},{16,4},{20,0},{24,12},{28,8},{1,21},{... | collective-permute-start | bytes 49160 | tf_op jit(solution)/shard_map/ppermute | solution.py:343
  74.6 5.9 %collective-permute-start.28 = (f32[192,128]{1,0:T(8,128)}, f32[192,128]{1,0:T(8,128)S(1)}, u32[]{:S(2)}, u32[]{:S(2)}) collective-permute-start(f32[192,128]{1,0:T(8,128)} %get-tuple-element.115), channel_id=1, source_target_pairs={{0,8},{4,12},{8,0},{12,4},{16,24},{20,28},{24,16},{28,20},{1,9},{5... | collective-permute-start | bytes 294920 | tf_op jit(solution)/shard_map/ppermute | solution.py:343
  76.1 13.3 %collective-permute-start.22 = (f32[208,128]{1,0:T(8,128)}, f32[208,128]{1,0:T(8,128)S(1)}, u32[]{:S(2)}, u32[]{:S(2)}) collective-permute-start(f32[208,128]{1,0:T(8,128)} %get-tuple-element.105), channel_id=1, source_target_pairs={{0,8},{4,12},{8,0},{12,4},{16,24},{20,28},{24,16},{28,20},{1,9},{5... | collective-permute-start | bytes 319496 | tf_op jit(solution)/shard_map/ppermute | solution.py:343
  81.4 9.0 %collective-permute-start.29 = (f32[192,128]{1,0:T(8,128)S(1)}, f32[192,128]{1,0:T(8,128)S(1)}, u32[]{:S(2)}, u32[]{:S(2)}) collective-permute-start(f32[192,128]{1,0:T(8,128)S(1)} %add.32), channel_id=1, source_target_pairs={{0,1},{1,0},{2,3},{3,2},{4,5},{5,4},{6,7},{7,6},{8,9},{9,8},{10,11... | collective-permute-start | bytes 294920 | tf_op jit(solution)/shard_map/ppermute | solution.py:349
  83.7 1.9 %collective-permute-start.16 = (f32[128,128]{1,0:T(8,128)}, f32[128,128]{1,0:T(8,128)S(1)}, u32[]{:S(2)}, u32[]{:S(2)}) collective-permute-start(f32[128,128]{1,0:T(8,128)} %get-tuple-element.95), channel_id=1, source_target_pairs={{0,4},{4,0},{8,12},{12,8},{16,20},{20,16},{24,28},{28,24},{1,5},{5... | collective-permute-start | bytes 196616 | tf_op jit(solution)/shard_map/ppermute | solution.py:343
  83.7 5.2 %collective-permute-start.17 = (f32[128,128]{1,0:T(8,128)}, f32[128,128]{1,0:T(8,128)S(1)}, u32[]{:S(2)}, u32[]{:S(2)}) collective-permute-start(f32[128,128]{1,0:T(8,128)} %get-tuple-element.96), channel_id=1, source_target_pairs={{0,16},{4,20},{8,24},{12,28},{16,0},{20,4},{24,8},{28,12},{1,17},{... | collective-permute-start | bytes 196616 | tf_op jit(solution)/shard_map/ppermute | solution.py:343
  84.6 4.8 %collective-permute-start.18 = (f32[128,128]{1,0:T(8,128)}, f32[128,128]{1,0:T(8,128)S(1)}, u32[]{:S(2)}, u32[]{:S(2)}) collective-permute-start(f32[128,128]{1,0:T(8,128)} %get-tuple-element.97), channel_id=1, source_target_pairs={{0,20},{4,16},{8,28},{12,24},{16,4},{20,0},{24,12},{28,8},{1,21},{... | collective-permute-start | bytes 196616 | tf_op jit(solution)/shard_map/ppermute | solution.py:343
  85.6 6.6 %copy-start.27 = (f32[128,128]{1,0:T(8,128)}, f32[128,128]{1,0:T(8,128)S(1)}, u32[]{:S(2)}) copy-start(f32[128,128]{1,0:T(8,128)S(1)} %collective-permute-done.16.refs_1_) | copy-start | bytes 196612
  88.9 3.3 %copy-start.28 = (f32[128,128]{1,0:T(8,128)}, f32[128,128]{1,0:T(8,128)S(1)}, u32[]{:S(2)}) copy-start(f32[128,128]{1,0:T(8,128)S(1)} %collective-permute-done.17.refs_2_) | copy-start | bytes 196612
  89.4 2.8 %copy-start.29 = (f32[128,128]{1,0:T(8,128)}, f32[128,128]{1,0:T(8,128)S(1)}, u32[]{:S(2)}) copy-start(f32[128,128]{1,0:T(8,128)S(1)} %collective-permute-done.18.refs_3_) | copy-start | bytes 196612
  90.3 5.6 %collective-permute-start.23 = (f32[208,128]{1,0:T(8,128)S(1)}, f32[208,128]{1,0:T(8,128)S(1)}, u32[]{:S(2)}, u32[]{:S(2)}) collective-permute-start(f32[208,128]{1,0:T(8,128)S(1)} %add.29), channel_id=1, source_target_pairs={{0,1},{1,0},{2,3},{3,2},{4,5},{5,4},{6,7},{7,6},{8,9},{9,8},{10,11... | collective-permute-start | bytes 319496 | tf_op jit(solution)/shard_map/ppermute | solution.py:349
  90.4 7.3 %collective-permute-start.30 = (f32[192,128]{1,0:T(8,128)S(1)}, f32[192,128]{1,0:T(8,128)S(1)}, u32[]{:S(2)}, u32[]{:S(2)}) collective-permute-start(f32[192,128]{1,0:T(8,128)S(1)} %add.33), channel_id=1, source_target_pairs={{0,3},{1,2},{2,1},{3,0},{4,7},{5,6},{6,5},{7,4},{8,11},{9,10},{10,... | collective-permute-start | bytes 294920 | tf_op jit(solution)/shard_map/ppermute | solution.py:349
  95.9 6.7 %collective-permute-start.24 = (f32[208,128]{1,0:T(8,128)S(1)}, f32[208,128]{1,0:T(8,128)S(1)}, u32[]{:S(2)}, u32[]{:S(2)}) collective-permute-start(f32[208,128]{1,0:T(8,128)S(1)} %add.30), channel_id=1, source_target_pairs={{0,3},{1,2},{2,1},{3,0},{4,7},{5,6},{6,5},{7,4},{8,11},{9,10},{10,... | collective-permute-start | bytes 319496 | tf_op jit(solution)/shard_map/ppermute | solution.py:349
  97.7 14.5 %copy-start.4 = (f32[192,128]{1,0:T(8,128)}, f32[192,128]{1,0:T(8,128)S(1)}, u32[]{:S(2)}) copy-start(f32[192,128]{1,0:T(8,128)S(1)} %add.34.refs_4_) | copy-start | bytes 294916
  97.8 6.7 %collective-permute-start.40 = (f32[192,128]{1,0:T(8,128)S(1)}, f32[192,128]{1,0:T(8,128)S(1)}, u32[]{:S(2)}, u32[]{:S(2)}) collective-permute-start(f32[192,128]{1,0:T(8,128)S(1)} %add.34.refs_4_), channel_id=1, source_target_pairs={{0,24},{4,28},{8,16},{12,20},{16,8},{20,12},{24,0},{28,4},{1,25},{... | collective-permute-start | bytes 294920 | tf_op jit(solution)/shard_map/ppermute | solution.py:343
  99.6 6.1 %collective-permute-start.38 = (f32[192,128]{1,0:T(8,128)S(1)}, f32[192,128]{1,0:T(8,128)S(1)}, u32[]{:S(2)}, u32[]{:S(2)}) collective-permute-start(f32[192,128]{1,0:T(8,128)S(1)} %add.34.refs_4_), channel_id=1, source_target_pairs={{0,8},{4,12},{8,0},{12,4},{16,24},{20,28},{24,16},{28,20},{1,9},{5... | collective-permute-start | bytes 294920 | tf_op jit(solution)/shard_map/ppermute | solution.py:343
  100.1 6.2 %collective-permute-start.32 = (f32[192,128]{1,0:T(8,128)S(1)}, f32[192,128]{1,0:T(8,128)S(1)}, u32[]{:S(2)}, u32[]{:S(2)}) collective-permute-start(f32[192,128]{1,0:T(8,128)S(1)} %add.34.refs_4_), channel_id=1, source_target_pairs={{0,16},{4,20},{8,24},{12,28},{16,0},{20,4},{24,8},{28,12},{1,17},{... | collective-permute-start | bytes 294920 | tf_op jit(solution)/shard_map/ppermute | solution.py:343
  101.3 5.1 %collective-permute-start.31 = (f32[192,128]{1,0:T(8,128)S(1)}, f32[192,128]{1,0:T(8,128)S(1)}, u32[]{:S(2)}, u32[]{:S(2)}) collective-permute-start(f32[192,128]{1,0:T(8,128)S(1)} %add.34.refs_4_), channel_id=1, source_target_pairs={{0,4},{4,0},{8,12},{12,8},{16,20},{20,16},{24,28},{28,24},{1,5},{5... | collective-permute-start | bytes 294920 | tf_op jit(solution)/shard_map/ppermute | solution.py:343
  102.6 9.7 %copy-start.3 = (f32[208,128]{1,0:T(8,128)}, f32[208,128]{1,0:T(8,128)S(1)}, u32[]{:S(2)}) copy-start(f32[208,128]{1,0:T(8,128)S(1)} %add.31.refs_0_) | copy-start | bytes 319492
  102.6 6.3 %collective-permute-start.36 = (f32[208,128]{1,0:T(8,128)S(1)}, f32[208,128]{1,0:T(8,128)S(1)}, u32[]{:S(2)}, u32[]{:S(2)}) collective-permute-start(f32[208,128]{1,0:T(8,128)S(1)} %add.31.refs_0_), channel_id=1, source_target_pairs={{0,24},{4,28},{8,16},{12,20},{16,8},{20,12},{24,0},{28,4},{1,25},{... | collective-permute-start | bytes 319496 | tf_op jit(solution)/shard_map/ppermute | solution.py:343
  104.5 7.8 %copy-start.17 = (f32[192,128]{1,0:T(8,128)}, f32[192,128]{1,0:T(8,128)S(1)}, u32[]{:S(2)}) copy-start(f32[192,128]{1,0:T(8,128)S(1)} %collective-permute-done.40.refs_14_) | copy-start | bytes 294916
  104.5 5.0 %collective-permute-start.34 = (f32[208,128]{1,0:T(8,128)S(1)}, f32[208,128]{1,0:T(8,128)S(1)}, u32[]{:S(2)}, u32[]{:S(2)}) collective-permute-start(f32[208,128]{1,0:T(8,128)S(1)} %add.31.refs_0_), channel_id=1, source_target_pairs={{0,8},{4,12},{8,0},{12,4},{16,24},{20,28},{24,16},{28,20},{1,9},{5... | collective-permute-start | bytes 319496 | tf_op jit(solution)/shard_map/ppermute | solution.py:343
  105.7 6.6 %copy-start.18 = (f32[192,128]{1,0:T(8,128)}, f32[192,128]{1,0:T(8,128)S(1)}, u32[]{:S(2)}) copy-start(f32[192,128]{1,0:T(8,128)S(1)} %collective-permute-done.38.refs_12_) | copy-start | bytes 294916
  105.7 4.7 %collective-permute-start.26 = (f32[208,128]{1,0:T(8,128)S(1)}, f32[208,128]{1,0:T(8,128)S(1)}, u32[]{:S(2)}, u32[]{:S(2)}) collective-permute-start(f32[208,128]{1,0:T(8,128)S(1)} %add.31.refs_0_), channel_id=1, source_target_pairs={{0,16},{4,20},{8,24},{12,28},{16,0},{20,4},{24,8},{28,12},{1,17},{... | collective-permute-start | bytes 319496 | tf_op jit(solution)/shard_map/ppermute | solution.py:343
  106.4 5.9 %copy-start.19 = (f32[192,128]{1,0:T(8,128)}, f32[192,128]{1,0:T(8,128)S(1)}, u32[]{:S(2)}) copy-start(f32[192,128]{1,0:T(8,128)S(1)} %collective-permute-done.32.refs_6_) | copy-start | bytes 294916
  106.4 4.0 %collective-permute-start.25 = (f32[208,128]{1,0:T(8,128)S(1)}, f32[208,128]{1,0:T(8,128)S(1)}, u32[]{:S(2)}, u32[]{:S(2)}) collective-permute-start(f32[208,128]{1,0:T(8,128)S(1)} %add.31.refs_0_), channel_id=1, source_target_pairs={{0,4},{4,0},{8,12},{12,8},{16,20},{20,16},{24,28},{28,24},{1,5},{5... | collective-permute-start | bytes 319496 | tf_op jit(solution)/shard_map/ppermute | solution.py:343
  106.4 5.9 %copy-start.20 = (f32[192,128]{1,0:T(8,128)}, f32[192,128]{1,0:T(8,128)S(1)}, u32[]{:S(2)}) copy-start(f32[192,128]{1,0:T(8,128)S(1)} %collective-permute-done.31.refs_5_) | copy-start | bytes 294916
  106.4 4.5 %collective-permute-start.41 = (f32[192,128]{1,0:T(8,128)S(1)}, f32[192,128]{1,0:T(8,128)S(1)}, u32[]{:S(2)}, u32[]{:S(2)}) collective-permute-start(f32[192,128]{1,0:T(8,128)S(1)} %collective-permute-done.40.refs_14_), channel_id=1, source_target_pairs={{0,4},{4,0},{8,12},{12,8},{16,20},{20,16},{24,28},{28,24},{1,5},{5... | collective-permute-start | bytes 294920 | tf_op jit(solution)/shard_map/ppermute | solution.py:343
  108.9 3.4 %copy-start.10 = (f32[208,128]{1,0:T(8,128)}, f32[208,128]{1,0:T(8,128)S(1)}, u32[]{:S(2)}) copy-start(f32[208,128]{1,0:T(8,128)S(1)} %collective-permute-done.36.refs_10_) | copy-start | bytes 319492
  108.9 3.3 %collective-permute-start.37 = (f32[208,128]{1,0:T(8,128)S(1)}, f32[208,128]{1,0:T(8,128)S(1)}, u32[]{:S(2)}, u32[]{:S(2)}) collective-permute-start(f32[208,128]{1,0:T(8,128)S(1)} %collective-permute-done.36.refs_10_), channel_id=1, source_target_pairs={{0,4},{4,0},{8,12},{12,8},{16,20},{20,16},{24,28},{28,24},{1,5},{5... | collective-permute-start | bytes 319496 | tf_op jit(solution)/shard_map/ppermute | solution.py:343
  109.4 2.9 %copy-start.11 = (f32[208,128]{1,0:T(8,128)}, f32[208,128]{1,0:T(8,128)S(1)}, u32[]{:S(2)}) copy-start(f32[208,128]{1,0:T(8,128)S(1)} %collective-permute-done.34.refs_8_) | copy-start | bytes 319492
  109.4 2.8 %collective-permute-start.35 = (f32[208,128]{1,0:T(8,128)S(1)}, f32[208,128]{1,0:T(8,128)S(1)}, u32[]{:S(2)}, u32[]{:S(2)}) collective-permute-start(f32[208,128]{1,0:T(8,128)S(1)} %collective-permute-done.34.refs_8_), channel_id=1, source_target_pairs={{0,4},{4,0},{8,12},{12,8},{16,20},{20,16},{24,28},{28,24},{1,5},{5... | collective-permute-start | bytes 319496 | tf_op jit(solution)/shard_map/ppermute | solution.py:343
  110.4 1.9 %copy-start.12 = (f32[208,128]{1,0:T(8,128)}, f32[208,128]{1,0:T(8,128)S(1)}, u32[]{:S(2)}) copy-start(f32[208,128]{1,0:T(8,128)S(1)} %collective-permute-done.26.refs_2_) | copy-start | bytes 319492
  110.4 1.9 %collective-permute-start.27 = (f32[208,128]{1,0:T(8,128)S(1)}, f32[208,128]{1,0:T(8,128)S(1)}, u32[]{:S(2)}, u32[]{:S(2)}) collective-permute-start(f32[208,128]{1,0:T(8,128)S(1)} %collective-permute-done.26.refs_2_), channel_id=1, source_target_pairs={{0,4},{4,0},{8,12},{12,8},{16,20},{20,16},{24,28},{28,24},{1,5},{5... | collective-permute-start | bytes 319496 | tf_op jit(solution)/shard_map/ppermute | solution.py:343
  110.4 1.9 %copy-start.13 = (f32[208,128]{1,0:T(8,128)}, f32[208,128]{1,0:T(8,128)S(1)}, u32[]{:S(2)}) copy-start(f32[208,128]{1,0:T(8,128)S(1)} %collective-permute-done.25.refs_1_) | copy-start | bytes 319492
  110.4 1.4 %collective-permute-start.39 = (f32[192,128]{1,0:T(8,128)S(1)}, f32[192,128]{1,0:T(8,128)S(1)}, u32[]{:S(2)}, u32[]{:S(2)}) collective-permute-start(f32[192,128]{1,0:T(8,128)S(1)} %collective-permute-done.38.refs_12_), channel_id=1, source_target_pairs={{0,4},{4,0},{8,12},{12,8},{16,20},{20,16},{24,28},{28,24},{1,5},{5... | collective-permute-start | bytes 294920 | tf_op jit(solution)/shard_map/ppermute | solution.py:343
  110.9 1.3 %collective-permute-start.33 = (f32[192,128]{1,0:T(8,128)S(1)}, f32[192,128]{1,0:T(8,128)S(1)}, u32[]{:S(2)}, u32[]{:S(2)}) collective-permute-start(f32[192,128]{1,0:T(8,128)S(1)} %collective-permute-done.32.refs_6_), channel_id=1, source_target_pairs={{0,4},{4,0},{8,12},{12,8},{16,20},{20,16},{24,28},{28,24},{1,5},{5... | collective-permute-start | bytes 294920 | tf_op jit(solution)/shard_map/ppermute | solution.py:343
  (15 other events, 11.8 us)
